TPU v7x, 256 devices: a whole 4x4x8 slice. The times are simulated.
256 devices in a mesh: fsdp: 8 (over z_hi, y), tensor: 32 (over x, z_lo, core).
Axes of the slice: x: 4, y: 4, z: 8 (z_hi: 2, z_lo: 4; z = z_hi * 4 + z_lo), core: 2. Of those that a mesh axis runs over, the one named last changes fastest.
Arguments:
- momentum: bfloat16 [8192, 28672], P('fsdp', 'tensor'), may hold values from -6 to 6
- gradient: bfloat16 [8192, 28672], P('fsdp', 'tensor'), may hold values from -4 to 4
- factor: float32 [28672, 512], P('tensor', 'fsdp'), may hold values from -0.03125 to 0.03125
Outputs:
- new_momentum: bfloat16 [8192, 28672], P('fsdp', 'tensor')
- new_factor: float32 [28672, 512], P('tensor', 'fsdp')
- update: bfloat16 [8192, 28672], P('fsdp', 'tensor')
All inputs are finite; a program needn't handle non-finite values.
Results may differ from a plain program's by a relative error of at most 0.017.
Values may be sent and summed in bfloat16 or wider, within the bound.
No kernel may reach another device: no remote copies, remote signals or barrier semaphores. Data moves between devices by JAX's collectives and lax.ppermute only.
A program may use at most 64 MiB of HBM per device.

v0:
```python
import math

import jax
import jax.numpy as jnp
from jax import lax
from jax.experimental import pallas as pl
from jax.experimental.pallas import tpu as pltpu
from jax.sharding import Mesh
from jax.sharding import PartitionSpec as P

D = 8192
FF = 28672
R = 512
FAR = 16
BLOCK = 128
BLOCKS = R // BLOCK
PAIRS = [(i, j) for i in range(BLOCKS) for j in range(i + 1)]
SHARE = len(PAIRS) * BLOCK // (2 * FAR)
SUB = 8
TENSOR = ("x", "z_lo", "core")

decay_rate = 0.95
epsilon = 1e-06
f32 = jnp.float32
bf16 = jnp.bfloat16


def product(left, right, left_dim, right_dim):
    return lax.dot_general(left, right, (((left_dim,), (right_dim,)), ((), ())), preferred_element_type=f32)


def added(terms):
    while len(terms) > 1:
        terms = [
            terms[i] + terms[i + 1] if i + 1 < len(terms) else terms[i] for i in range(0, len(terms), 2)
        ]
    return terms[0]


def spread(value):
    return jnp.broadcast_to(value, (SUB, BLOCK))


def small_inverse(entries):
    rest = [row[:] for row in entries]
    inverse = [None] * SUB
    upper = [[None] * SUB for _ in range(SUB)]
    for j in range(SUB):
        inverse[j] = lax.rsqrt(rest[j][j])
        for k in range(j + 1, SUB):
            upper[j][k] = rest[j][k] * inverse[j]
        for i in range(j + 1, SUB):
            for k in range(i, SUB):
                rest[i][k] = rest[i][k] - upper[j][i] * upper[j][k]
    result = [[None] * SUB for _ in range(SUB)]
    for j in range(SUB):
        result[j][j] = inverse[j]
        for i in range(j + 1, SUB):
            total = upper[j][i] * result[j][j]
            for k in range(j + 1, i):
                total = total + upper[k][i] * result[k][j]
            result[i][j] = -(inverse[i] * total)
    return result


def in_three(value):
    first = value.astype(bf16)
    rest = value - first.astype(f32)
    second = rest.astype(bf16)
    return first, second, (rest - second.astype(f32)).astype(bf16)


def exact(left, right, left_dim, right_dim):
    a, b, c = in_three(left)
    d, e, f = in_three(right)
    lefts = jnp.concatenate([a, a, b, b, a, c], axis=left_dim)
    rights = jnp.concatenate([d, e, d, e, f, d], axis=right_dim)
    return product(lefts, rights, left_dim, right_dim)


def factor_block(held):
    sub = lax.broadcasted_iota(jnp.int32, (SUB, BLOCK), 0)
    lane = lax.broadcasted_iota(jnp.int32, (SUB, BLOCK), 1)
    lane_row = lax.broadcasted_iota(jnp.int32, (1, BLOCK), 1)
    rows, following = held[:SUB, :], held[SUB : 2 * SUB, :]
    for lo in range(0, BLOCK, SUB):
        inside = (lane >= lo) & (lane < lo + SUB)
        lanes = [spread(rows[:, lo + k : lo + k + 1]) for k in range(SUB)]
        entries = [[spread(lanes[k][i : i + 1, :]) if k >= i else None for k in range(SUB)] for i in range(SUB)]
        inverse = small_inverse(entries)
        bare = [
            jnp.where(lane == lo + k, 1.0, jnp.where(inside, 0.0, spread(rows[k : k + 1, :]))) for k in range(SUB)
        ]
        done = [added([inverse[i][k] * bare[k] for k in range(i + 1)]) for i in range(SUB)]
        packed = done[0]
        for i in range(1, SUB):
            packed = jnp.where(sub == i, done[i], packed)
        held[lo : lo + SUB, :] = packed
        if lo + SUB < BLOCK:
            weights = [added([inverse[m][k] * done[m] for m in range(k, SUB)]) for k in range(SUB)]

            def brought(later):
                terms = [spread(later[:, lo + k : lo + k + 1]) * weights[k] for k in range(SUB)]
                return jnp.where(inside, 0.0, later) - added(terms)

            rows = brought(following)
        if lo + 2 * SUB < BLOCK:
            following = brought(held[lo + 2 * SUB : lo + 3 * SUB, :])
        if lo + 3 * SUB < BLOCK:
            change = exact(packed, packed, 0, 0)
            kept = jnp.where((lane_row >= lo) & (lane_row < lo + SUB), 0.0, held[lo + 3 * SUB :, :])
            held[lo + 3 * SUB :, :] = kept - change[lo + 3 * SUB :, :]


FIRST = {pair: n * BLOCK for n, pair in enumerate(PAIRS)}


def eliminate(b, own, gram, inverse):
    def block(i, j):
        return gram[FIRST[i, j] : FIRST[i, j] + BLOCK, :]

    lo, hi = b * BLOCK, (b + 1) * BLOCK
    if b:
        inverse[lo:hi, :lo] = exact(own, inverse[lo:hi, :lo], 1, 0)
    inverse[lo:hi, lo:hi] = own
    lower = {i: exact(block(i, b), own, 1, 1) for i in range(b + 1, BLOCKS)}
    for i in range(b + 1, BLOCKS):
        for j in range(b + 1, i + 1):
            gram[FIRST[i, j] : FIRST[i, j] + BLOCK, :] = block(i, j) - exact(lower[i], lower[j], 1, 1)
        into = slice(i * BLOCK, (i + 1) * BLOCK)
        inverse[into, :hi] = inverse[into, :hi] - exact(lower[i], inverse[lo:hi, :hi], 1, 0)


def inverse_kernel(place_ref, own_ref, other_ref, high_ref, low_ref, gram, inverse, held):
    for n in range(2 * FAR):
        source = own_ref if n < FAR else other_ref
        into = pl.multiple_of(place_ref[n] * SHARE, SUB)
        gram[pl.ds(into, SHARE), :] = source[(n % FAR) * SHARE : (n % FAR + 1) * SHARE, :]
    inverse[...] = jnp.zeros_like(inverse)
    row = lax.broadcasted_iota(jnp.int32, (BLOCK, BLOCK), 0)
    column = lax.broadcasted_iota(jnp.int32, (BLOCK, BLOCK), 1)

    @pl.loop(0, BLOCKS)
    def _(b):
        first = pl.multiple_of((b * (b + 1) // 2 + b) * BLOCK, BLOCK)
        held[...] = gram[pl.ds(first, BLOCK), :]
        factor_block(held)
        own = jnp.where(column <= row, held[...], 0.0)
        for step in range(BLOCKS):

            @pl.when(b == step)
            def _():
                eliminate(step, own, gram, inverse)

    high = inverse[...].astype(bf16)
    high_ref[...] = high
    low_ref[...] = (inverse[...] - high.astype(f32)).astype(bf16)


def kernel_call(kernel, place, inputs, outputs, scratch, flops):
    whole = pl.BlockSpec(memory_space=pltpu.VMEM)
    return pl.pallas_call(
        kernel,
        out_shape=outputs,
        in_specs=[pl.BlockSpec(memory_space=pltpu.SMEM)] + [whole] * len(inputs),
        out_specs=[whole] * len(outputs),
        scratch_shapes=[pltpu.VMEM(*one) for one in scratch],
        compiler_params=pltpu.CompilerParams(vmem_limit_bytes=12 << 20),
        cost_estimate=pl.CostEstimate(flops=flops, bytes_accessed=2 << 20, transcendentals=0),
    )(place, *inputs)


def inverse_factor(place, own, other):
    return kernel_call(
        inverse_kernel,
        place,
        (own, other),
        [jax.ShapeDtypeStruct((R, R), bf16)] * 2,
        [((len(PAIRS) * BLOCK, BLOCK), f32), ((R, R), f32), ((BLOCK, BLOCK), f32)],
        20 * R**3,
    )


def arrange(place, inputs, rows):
    def kernel(place_ref, *refs):
        n = 0
        for source in refs[:-1]:
            for lo in range(0, source.shape[0], rows):
                into = pl.multiple_of(place_ref[n] * rows, rows)
                refs[-1][pl.ds(into, rows), :] = source[lo : lo + rows, :]
                n += 1

    height = sum(value.shape[0] for value in inputs)
    output = jax.ShapeDtypeStruct((height, inputs[0].shape[1]), inputs[0].dtype)
    return kernel_call(kernel, place, inputs, [output], [], 1 << 20)[0]


def right_kernel(place_ref, high_ref, low_ref, *refs):
    pieces, (right_ref, own_ref, sums_ref, raw, whole) = refs[:4], refs[4:]
    quarter = R // 4
    for n in range(4):
        into = pl.multiple_of(place_ref[n] * quarter, quarter)
        raw[pl.ds(into, quarter), :] = pieces[n][...]
    for lo in range(0, R, BLOCK):
        band = slice(lo, lo + BLOCK)
        right = product(high_ref[band, :], raw[...], 1, 0) + product(low_ref[band, :], raw[...], 1, 0)
        whole[band, :] = right
        right_ref[band, :] = right.astype(bf16)
        square = right * right
        folded = added([square[:, at : at + BLOCK] for at in range(0, right.shape[1], BLOCK)])
        sums_ref[:, band] = jnp.sum(folded.T, axis=0, keepdims=True)
    rows = own_ref.shape[0]
    own_ref[...] = whole[pl.ds(pl.multiple_of(place_ref[4] * rows, rows), rows), :]


def right_side(place, high, low, pieces, rows):
    width = pieces[0].shape[1]
    return kernel_call(
        right_kernel,
        place,
        (high, low, *pieces),
        [
            jax.ShapeDtypeStruct((R, width), bf16),
            jax.ShapeDtypeStruct((rows, width), f32),
            jax.ShapeDtypeStruct((1, R), f32),
        ],
        [((R, width), bf16), ((R, width), f32)],
        4 * R * R * width,
    )


def update_kernel(place_ref, left_ref, right_ref, own_ref, inverse_ref, update_ref, factor_ref, column):
    @pl.when(pl.program_id(0) == 0)
    def _():
        rows = own_ref.shape[0]
        column[...] = jnp.broadcast_to(inverse_ref[...], (BLOCK, R)).T
        scale = column[pl.ds(pl.multiple_of(place_ref[4] * rows, rows), rows), :]
        for at in range(0, own_ref.shape[1], BLOCK):
            factor_ref[:, at : at + BLOCK] = own_ref[:, at : at + BLOCK] * scale

    scaled = (left_ref[...].astype(f32) * inverse_ref[...]).astype(bf16)
    update_ref[...] = (product(scaled, right_ref[...], 1, 0) * math.sqrt(D * FF / R)).astype(bf16)


def update_side(place, left, right, own, inverse):
    height, width = left.shape[0], right.shape[1]
    band = height // 4

    def fixed(value):
        return pl.BlockSpec(value.shape, lambda i: (0, 0))

    return pl.pallas_call(
        update_kernel,
        grid=(4,),
        out_shape=[jax.ShapeDtypeStruct((height, width), bf16), jax.ShapeDtypeStruct(own.shape, f32)],
        in_specs=[
            pl.BlockSpec(memory_space=pltpu.SMEM),
            pl.BlockSpec((band, R), lambda i: (i, 0)),
            fixed(right),
            fixed(own),
            fixed(inverse),
        ],
        out_specs=[pl.BlockSpec((band, width), lambda i: (i, 0)), fixed(own)],
        scratch_shapes=[pltpu.VMEM((R, BLOCK), f32)],
        compiler_params=pltpu.CompilerParams(vmem_limit_bytes=12 << 20),
        cost_estimate=pl.CostEstimate(flops=2 * R * height * width, bytes_accessed=4 << 20, transcendentals=0),
    )(place, left, right, own, inverse)


def from_everyone(value, axis):
    length = lax.axis_size(axis)
    return lax.all_to_all(jnp.broadcast_to(value[None], (length, *value.shape)), axis, 0, 0, tiled=True)


def from_ahead(value, axis, steps):
    length = lax.axis_size(axis)
    return lax.ppermute(value, axis, [(i, (i - steps) % length) for i in range(length)])


def ahead(value, axis):
    return [value] + [from_ahead(value, axis, steps) for steps in range(1, lax.axis_size(axis))]


def exchanged(value, axis, index):
    count = lax.axis_size(axis)
    length = value.shape[0] // count
    pieces = [lax.dynamic_slice_in_dim(value, (index + k) % count * length, length, 0) for k in range(count)]
    return [pieces[0]] + [from_ahead(pieces[count - k], axis, k) for k in range(1, count)]


def total(pieces):
    return sum((value.astype(f32) for value in pieces[1:]), pieces[0].astype(f32))


def on_device(momentum, gradient, factor):
    z_hi, y, x, z_lo, core = (lax.axis_index(name) for name in ("z_hi", "y", "x", "z_lo", "core"))
    columns = factor.shape[1]
    gram_place = jnp.stack(
        [(core + c) % 2 * FAR + (x + j) % 4 * 4 + i for c in range(2) for j in range(4) for i in range(4)]
    ).astype(jnp.int32)
    core_place = jnp.stack([core, 1 - core]).astype(jnp.int32)
    fsdp_place = jnp.stack([(z_hi + h) % 2 * 4 + (y + k) % 4 for h in range(2) for k in range(4)]).astype(jnp.int32)
    row_group = z_hi * 4 + y
    right_place = jnp.stack([(y + k) % 4 for k in range(4)] + [row_group]).astype(jnp.int32)

    lowered = factor.T.astype(bf16)
    near = ahead(lowered, "y")
    across = ahead(from_ahead(lowered, "z_hi", 1), "y")
    all_lowered = arrange(fsdp_place, near + across, columns)
    blended = (momentum.astype(f32) + gradient.astype(f32)).astype(bf16)
    half = blended.shape[0] // 2
    own_rows = lax.dynamic_slice_in_dim(blended, core * half, half, 0)
    other_rows = lax.dynamic_slice_in_dim(blended, (1 - core) * half, half, 0)

    sent = product(other_rows, all_lowered, 1, 1).astype(bf16)
    arrived = from_ahead(sent, "core", 1)
    partial_left = (product(own_rows, all_lowered, 1, 1) + arrived.astype(f32)).astype(bf16)
    left_line = total(exchanged(partial_left, "x", x)).astype(bf16)
    left_rows = total(exchanged(left_line, "z_lo", z_lo)).astype(bf16)
    own_left = from_everyone(left_rows, ("x", "z_lo")).reshape(half, R)
    other_left = from_ahead(own_left, "core", 1)

    local_gram = product(own_left, own_left, 0, 0) + product(other_left, other_left, 0, 0)
    packed = jnp.concatenate(
        [local_gram[i * BLOCK : (i + 1) * BLOCK, j * BLOCK : (j + 1) * BLOCK] for i, j in PAIRS]
    )
    piece = lax.dynamic_slice_in_dim(packed, (core * FAR + x * 4 + z_lo) * SHARE, SHARE, 0)
    summed = jnp.sum(from_everyone(piece, ("z_hi", "y")), axis=0)

    left_factor = arrange(core_place, (own_left, other_left), half)
    partial_right = product(left_factor, blended, 0, 0).astype(bf16)
    received = exchanged(partial_right, "y", y)

    gram_line = from_everyone(summed, "z_lo").reshape(4 * SHARE, BLOCK)
    gram_line, *received = lax.optimization_barrier((gram_line, *received))
    right_rows = total(received).astype(bf16)
    gram_line, right_rows = lax.optimization_barrier((gram_line, right_rows))
    opposite = from_ahead(right_rows, "z_hi", 1)
    opposite, *gram_lines = lax.optimization_barrier((opposite, *ahead(gram_line, "x")))
    own_gram = jnp.concatenate(gram_lines)
    other_gram = from_ahead(own_gram, "core", 1)
    right_rows = total([right_rows, opposite]).astype(bf16)
    other_gram, right_rows = lax.optimization_barrier((other_gram, right_rows))
    right_pieces = ahead(right_rows, "y")
    high, low = inverse_factor(gram_place, own_gram, other_gram)
    right_factor, own_right, own_sums = right_side(right_place, high, low, right_pieces, columns)

    last_left, own_sums = lax.optimization_barrier((left_factor, own_sums))
    square_sums = jnp.sum(from_everyone(own_sums, TENSOR), axis=(0, 1))
    orthonormal = (product(last_left, high, 1, 1) + product(last_left, low, 1, 1)).astype(bf16)
    taken = product(orthonormal, right_factor, 1, 0)
    new_momentum = (blended.astype(f32) - (1.0 - decay_rate) * taken).astype(bf16)
    inverse = lax.rsqrt(square_sums + epsilon)[None]
    update, own_factor = update_side(right_place, orthonormal, right_factor, own_right, inverse)
    return (new_momentum, own_factor.T, update)


def solution(mesh):
    torus = Mesh(mesh.devices.reshape(2, 4, 4, 4, 2), ("z_hi", "y", "x", "z_lo", "core"))
    fsdp = ("z_hi", "y")
    return jax.shard_map(
        on_device,
        mesh=torus,
        in_specs=(P(fsdp, TENSOR), P(fsdp, TENSOR), P(TENSOR, fsdp)),
        out_specs=(P(fsdp, TENSOR), P(TENSOR, fsdp), P(fsdp, TENSOR)),
        check_vma=False,
    )
```

profile of v0, /device:TPU:1, one launch (start us, length us, event | category | flops | bytes accessed | tf_op | source)
XLA Modules:
  0.0 160.0 jit_solution(15605546608185226410)
XLA Ops:
  0.6 1.0 convert_bitcast_fusion.refs_0_
  1.6 7.8 %collective-permute-start.3 = (bf16[64,896]{1,0:T(8,128)(2,1)S(1)}, bf16[64,896]{1,0:T(8,128)(2,1)S(1)}, u32[]{:S(2)}, u32[]{:S(2)}) collective-permute-start(bf16[64,896]{1,0:T(8,128)(2,1)S(1)} %convert_bitcast_fusion.refs_0_), channel_id=1, source_target_pairs={{0,128},{128,0},{1,129},{129,1},{2,130},{130,2},{3,131},{131,3},{4... | collective-permute-start | bytes 344072 | tf_op jit(solution)/shard_map/ppermute | solution.py:277
  9.4 1.3 collective-permute-start.2
  10.7 2.6 %collective-permute-start.1 = (bf16[64,896]{1,0:T(8,128)(2,1)S(1)}, bf16[64,896]{1,0:T(8,128)(2,1)S(1)}, u32[]{:S(2)}, u32[]{:S(2)}) collective-permute-start(bf16[64,896]{1,0:T(8,128)(2,1)S(1)} %convert_bitcast_fusion.refs_0_), channel_id=1, source_target_pairs={{0,64},{32,96},{64,0},{96,32},{1,65},{33,97},{65,1},{97,33},{2,66}... | collective-permute-start | bytes 344072 | tf_op jit(solution)/shard_map/ppermute | solution.py:277
  13.3 1.1 collective-permute-start
  14.8 1.4 collective-permute-start.5
  16.2 1.1 collective-permute-start.4
  17.3 3.7 %add_convert_fusion = bf16[1024,896]{1,0:T(8,128)(2,1)} fusion(bf16[1024,896]{1,0:T(8,128)(2,1)} %param.4, bf16[1024,896]{1,0:T(8,128)(2,1)} %param.3), kind=kLoop, calls=%fused_computation.1 | loop fusion | flops 3670016 | bytes 5505024 | tf_op jit(solution)/shard_map/convert_element_type | solution.py:310
  21.1 1.5 collective-permute-done.5.refs_6_
  24.0 2.3 %collective-permute-start.7 = (bf16[512,512]{1,0:T(8,128)(2,1)S(1)}, bf16[512,512]{1,0:T(8,128)(2,1)}, u32[]{:S(2)}, u32[]{:S(2)}) collective-permute-start(bf16[512,512]{1,0:T(8,128)(2,1)S(1)} %convolution_convert_fusion.1), channel_id=1, source_target_pairs={{0,1},{1,0},{2,3},{3,2},{4,5},{5,4},{6,7},{7,6},{8,9},{9,8},{10,11... | collective-permute-start | bytes 1572872 | tf_op jit(solution)/shard_map/ppermute | solution.py:277
  26.3 1.7 %collective-permute-done.7 = bf16[512,512]{1,0:T(8,128)(2,1)} collective-permute-done((bf16[512,512]{1,0:T(8,128)(2,1)S(1)}, bf16[512,512]{1,0:T(8,128)(2,1)}, u32[]{:S(2)}, u32[]{:S(2)}) %collective-permute-start.7) | collective-permute-done | bytes 524320 | tf_op jit(solution)/shard_map/ppermute | solution.py:277
  28.0 1.8 %fusion = bf16[512,512]{1,0:T(8,128)(2,1)S(1)} fusion(bf16[512,896]{1,0:T(8,128)(2,1)S(1)} %shard_map.58, bf16[512,512]{1,0:T(8,128)(2,1)} %collective-permute-done.7, bf16[1024,896]{1,0:T(8,128)(2,1)S(1)} %copy-done.3, s32[]{:T(128)S(6)} %select_n.272), kind=kOutput, calls=%fused_computation.7 | convolution fusion | flops 470548480 | bytes 2883588 | tf_op jit(solution)/shard_map/dot_general | solution.py:29
  29.8 2.6 %collective-permute-start.8 = (bf16[128,512]{1,0:T(8,128)(2,1)S(1)}, bf16[128,512]{1,0:T(8,128)(2,1)S(1)}, u32[]{:S(2)}, u32[]{:S(2)}) collective-permute-start(bf16[128,512]{1,0:T(8,128)(2,1)S(1)} %get-tuple-element.53), channel_id=1, source_target_pairs={{0,24},{8,0},{16,8},{24,16},{1,25},{9,1},{17,9},{25,17},{2,26},{10... | collective-permute-start | bytes 393224 | tf_op jit(solution)/shard_map/ppermute | solution.py:277
  32.4 1.7 %collective-permute-start.9 = (bf16[128,512]{1,0:T(8,128)(2,1)S(1)}, bf16[128,512]{1,0:T(8,128)(2,1)S(1)}, u32[]{:S(2)}, u32[]{:S(2)}) collective-permute-start(bf16[128,512]{1,0:T(8,128)(2,1)S(1)} %get-tuple-element.55), channel_id=1, source_target_pairs={{0,16},{8,24},{16,0},{24,8},{1,17},{9,25},{17,1},{25,9},{2,18},{10... | collective-permute-start | bytes 393224 | tf_op jit(solution)/shard_map/ppermute | solution.py:277
  34.1 0.8 collective-permute-done.8
  34.9 4.4 %collective-permute-done.10 = bf16[128,512]{1,0:T(8,128)(2,1)S(1)} collective-permute-done((bf16[128,512]{1,0:T(8,128)(2,1)S(1)}, bf16[128,512]{1,0:T(8,128)(2,1)S(1)}, u32[]{:S(2)}, u32[]{:S(2)}) %collective-permute-start.10) | collective-permute-done | bytes 131104 | tf_op jit(solution)/shard_map/ppermute | solution.py:277
  40.0 2.1 %collective-permute-start.11 = (bf16[32,512]{1,0:T(8,128)(2,1)S(1)}, bf16[32,512]{1,0:T(8,128)(2,1)S(1)}, u32[]{:S(2)}, u32[]{:S(2)}) collective-permute-start(bf16[32,512]{1,0:T(8,128)(2,1)S(1)} %get-tuple-element.56), channel_id=1, source_target_pairs={{0,6},{2,0},{4,2},{6,4},{1,7},{3,1},{5,3},{7,5},{8,14},{10,8},{12,... | collective-permute-start | bytes 98312 | tf_op jit(solution)/shard_map/ppermute | solution.py:277
  42.5 2.2 %collective-permute-start.12 = (bf16[32,512]{1,0:T(8,128)(2,1)S(1)}, bf16[32,512]{1,0:T(8,128)(2,1)S(1)}, u32[]{:S(2)}, u32[]{:S(2)}) collective-permute-start(bf16[32,512]{1,0:T(8,128)(2,1)S(1)} %get-tuple-element.58), channel_id=1, source_target_pairs={{0,4},{2,6},{4,0},{6,2},{1,5},{3,7},{5,1},{7,3},{8,12},{10,14},{12... | collective-permute-start | bytes 98312 | tf_op jit(solution)/shard_map/ppermute | solution.py:277
  44.7 2.0 %collective-permute-done.13 = bf16[32,512]{1,0:T(8,128)(2,1)S(1)} collective-permute-done((bf16[32,512]{1,0:T(8,128)(2,1)S(1)}, bf16[32,512]{1,0:T(8,128)(2,1)S(1)}, u32[]{:S(2)}, u32[]{:S(2)}) %collective-permute-start.13) | collective-permute-done | bytes 32800 | tf_op jit(solution)/shard_map/ppermute | solution.py:277
  46.8 20.5 %all_to_all.20 = bf16[16,32,512]{2,1,0:T(8,128)(2,1)S(1)} all-to-all(bf16[16,32,512]{2,1,0:T(8,128)(2,1)S(1)} %broadcast_in_dim.10), channel_id=1, replica_groups=mesh['z_hi'=2,'y'=4,'x'=4,'z_lo'=4,'core'=2] {'x','z_lo'}, dimensions={0} | all-to-all | bytes 1048576 | tf_op jit(solution)/shard_map/all_to_all | solution.py:272
  67.3 2.2 %collective-permute-start.14 = (bf16[512,512]{1,0:T(8,128)(2,1)S(1)}, bf16[512,512]{1,0:T(8,128)(2,1)S(1)}, u32[]{:S(2)}, u32[]{:S(2)}) collective-permute-start(bf16[512,512]{1,0:T(8,128)(2,1)S(1)} %bitcast.70), channel_id=1, source_target_pairs={{0,1},{1,0},{2,3},{3,2},{4,5},{5,4},{6,7},{7,6},{8,9},{9,8},{10,11... | collective-permute-start | bytes 1572872 | tf_op jit(solution)/shard_map/ppermute | solution.py:277
  70.1 1.0 collective-permute-done.14.refs_1_
  72.4 7.6 %all-to-all-start.1 = ((f32[8,40,128]{2,1,0:T(8,128)}), f32[8,40,128]{2,1,0:T(8,128)S(1)}, u32[]{:S(2)}, u32[]{:S(2)}) async-start(f32[8,40,128]{2,1,0:T(8,128)} %broadcast_in_dim.11), calls=%async_computation.1 | async-start | bytes 327680 | tf_op jit(solution)/shard_map/all_to_all | solution.py:272
  80.6 2.8 %convolution_convert_fusion = bf16[512,896]{1,0:T(8,128)(2,1)S(1)} fusion(bf16[1024,512]{1,0:T(8,128)(2,1)S(1)} %shard_map.59, bf16[1024,896]{1,0:T(8,128)(2,1)} %add_convert_fusion), kind=kOutput, calls=%fused_computation.3 | convolution fusion | flops 939982848 | bytes 3801088 | tf_op jit(solution)/shard_map/dot_general | solution.py:29
  83.5 1.5 collective-permute-start.17
  85.0 2.4 %collective-permute-start.16 = (bf16[128,896]{1,0:T(8,128)(2,1)S(1)}, bf16[128,896]{1,0:T(8,128)(2,1)S(1)}, u32[]{:S(2)}, u32[]{:S(2)}) collective-permute-start(bf16[128,896]{1,0:T(8,128)(2,1)S(1)} %get-tuple-element.50), channel_id=1, source_target_pairs={{0,64},{32,96},{64,0},{96,32},{1,65},{33,97},{65,1},{97,33},{2,66}... | collective-permute-start | bytes 688136 | tf_op jit(solution)/shard_map/ppermute | solution.py:277
  87.4 1.2 collective-permute-start.15
  88.6 1.0 all-to-all-done.1
  90.2 3.3 %all-to-all-start.2 = ((f32[4,40,128]{2,1,0:T(8,128)}), f32[4,40,128]{2,1,0:T(8,128)S(1)}, u32[]{:S(2)}, u32[]{:S(2)}) async-start(f32[4,40,128]{2,1,0:T(8,128)} %broadcast_in_dim.12), calls=%async_computation.2 | async-start | bytes 163840 | tf_op jit(solution)/shard_map/all_to_all | solution.py:272
  93.6 4.8 %collective-permute-done.16 = bf16[128,896]{1,0:T(8,128)(2,1)S(1)} collective-permute-done((bf16[128,896]{1,0:T(8,128)(2,1)S(1)}, bf16[128,896]{1,0:T(8,128)(2,1)S(1)}, u32[]{:S(2)}, u32[]{:S(2)}) %collective-permute-start.16) | collective-permute-done | bytes 229408 | tf_op jit(solution)/shard_map/ppermute | solution.py:277
  98.6 4.2 %collective-permute-start.18 = (bf16[128,896]{1,0:T(8,128)(2,1)S(1)}, bf16[128,896]{1,0:T(8,128)(2,1)S(1)}, u32[]{:S(2)}, u32[]{:S(2)}) collective-permute-start(bf16[128,896]{1,0:T(8,128)(2,1)S(1)} %add_convert_fusion.3), channel_id=1, source_target_pairs={{0,128},{128,0},{1,129},{129,1},{2,130},{130,2},{3,131},{131,3},{4... | collective-permute-start | bytes 688136 | tf_op jit(solution)/shard_map/ppermute | solution.py:277
  102.7 1.8 %collective-permute-start.20 = (f32[160,128]{1,0:T(8,128)S(1)}, f32[160,128]{1,0:T(8,128)S(1)}, u32[]{:S(2)}, u32[]{:S(2)}) collective-permute-start(f32[160,128]{1,0:T(8,128)S(1)} %bitcast.75), channel_id=1, source_target_pairs={{0,16},{8,24},{16,0},{24,8},{1,17},{9,25},{17,1},{25,9},{2,18},{10... | collective-permute-start | bytes 245768 | tf_op jit(solution)/shard_map/ppermute | solution.py:277
  104.5 0.9 collective-permute-start.19
  105.4 2.7 %collective-permute-done.21 = f32[160,128]{1,0:T(8,128)S(1)} collective-permute-done((f32[160,128]{1,0:T(8,128)S(1)}, f32[160,128]{1,0:T(8,128)S(1)}, u32[]{:S(2)}, u32[]{:S(2)}) %collective-permute-start.21) | collective-permute-done | bytes 81952 | tf_op jit(solution)/shard_map/ppermute | solution.py:277
  108.7 1.6 collective-permute-done.18
  110.3 3.1 %collective-permute-start.22 = (f32[640,128]{1,0:T(8,128)S(1)}, f32[640,128]{1,0:T(8,128)S(1)}, u32[]{:S(2)}, u32[]{:S(2)}) collective-permute-start(f32[640,128]{1,0:T(8,128)S(1)} %constant_dynamic-update-slice_fusion.own_ref), channel_id=1, source_target_pairs={{0,1},{1,0},{2,3},{3,2},{4,5},{5,4},{6,7},{7,6},{8,9},{9,8},{10,11... | collective-permute-start | bytes 983048 | tf_op jit(solution)/shard_map/ppermute | solution.py:277
  113.7 1.0 collective-permute-done.22.other_ref
  114.7 3.2 %collective-permute-start.25 = (bf16[128,896]{1,0:T(8,128)(2,1)S(1)}, bf16[128,896]{1,0:T(8,128)(2,1)S(1)}, u32[]{:S(2)}, u32[]{:S(2)}) collective-permute-start(bf16[128,896]{1,0:T(8,128)(2,1)S(1)} %add_convert_fusion.2.refs_0_), channel_id=1, source_target_pairs={{0,32},{32,64},{64,96},{96,0},{1,33},{33,65},{65,97},{97,1},{2,34}... | collective-permute-start | bytes 688136 | tf_op jit(solution)/shard_map/ppermute | solution.py:277
  117.9 2.5 %collective-permute-start.24 = (bf16[128,896]{1,0:T(8,128)(2,1)S(1)}, bf16[128,896]{1,0:T(8,128)(2,1)S(1)}, u32[]{:S(2)}, u32[]{:S(2)}) collective-permute-start(bf16[128,896]{1,0:T(8,128)(2,1)S(1)} %add_convert_fusion.2.refs_0_), channel_id=1, source_target_pairs={{0,64},{32,96},{64,0},{96,32},{1,65},{33,97},{65,1},{97,33},{2,66}... | collective-permute-start | bytes 688136 | tf_op jit(solution)/shard_map/ppermute | solution.py:277
  120.5 18.3 %shard_map.60 = (bf16[512,512]{1,0:T(8,128)(2,1)S(1)}, bf16[512,512]{1,0:T(8,128)(2,1)S(1)}) custom-call(s32[32]{0:T(128)S(1)} %stack.203.place_ref, f32[640,128]{1,0:T(8,128)S(1)} %constant_dynamic-update-slice_fusion.own_ref, f32[640,128]{1,0:T(8,128)S(1)} %collective-permute-done.22.other_ref), custom_call_target="tpu_custom_call" | custom-call | flops 2684354560 | bytes 2097152 | tf_op jit(solution)/shard_map/pallas_call | solution.py:162
  138.9 2.0 %shard_map.61 = (bf16[512,896]{1,0:T(8,128)(2,1)S(1)}, f32[64,896]{1,0:T(8,128)S(1)}, f32[1,512]{1,0:T(1,128)S(1)}) custom-call(s32[5]{0:T(128)S(1)} %stack.170.place_ref, bf16[512,512]{1,0:T(8,128)(2,1)S(1)} %get-tuple-element.39.high_ref, bf16[512,512]{1,0:T(8,128)(2,1)S(1)} %get-tuple-element.40.low_ref, bf16[128,896]{1,0:T(8,128)(2,1)S(1)} %add_convert_fusion.2.refs_0_, ...), custom_call_target="tpu_custom_call" | custom-call | flops 939524096 | bytes 2097152 | tf_op jit(solution)/shard_map/pallas_call | solution.py:162
  142.2 5.3 %all-to-all-start.3 = ((f32[32,1,512]{2,1,0:T(1,128)}), f32[32,1,512]{2,1,0:T(1,128)}, u32[]{:S(2)}, u32[]{:S(2)}) async-start(f32[32,1,512]{2,1,0:T(1,128)} %broadcast_in_dim.14), calls=%async_computation.3 | async-start | bytes 131072 | tf_op jit(solution)/shard_map/all_to_all | solution.py:272
  148.3 0.7 add_convert_fusion.1.left_ref
  149.0 0.7 copy-done.4
  149.8 2.5 %subtract_convert_fusion = bf16[1024,896]{1,0:T(8,128)(2,1)} fusion(bf16[1024,896]{1,0:T(8,128)(2,1)S(1)} %copy-done.4, bf16[1024,512]{1,0:T(8,128)(2,1)S(1)} %add_convert_fusion.1.left_ref, bf16[512,896]{1,0:T(8,128)(2,1)S(1)} %get-tuple-element.44.right_ref), kind=kOutput, calls=%fused_computation | convolution fusion | flops 943194112 | bytes 5636096 | tf_op jit(solution)/shard_map/dot_general | solution.py:29
  152.3 3.2 %all-to-all-done.3 = f32[32,1,512]{2,1,0:T(1,128)} async-done(((f32[32,1,512]{2,1,0:T(1,128)}), f32[32,1,512]{2,1,0:T(1,128)}, u32[]{:S(2)}, u32[]{:S(2)}) %all-to-all-start.3) | async-done | bytes 65568 | tf_op jit(solution)/shard_map/all_to_all | solution.py:272
  155.5 0.9 reduce_sum.19
  156.4 3.6 %shard_map.62 = (bf16[1024,896]{1,0:T(8,128)(2,1)}, f32[64,896]{1,0:T(8,128)}) custom-call(s32[5]{0:T(128)S(1)} %stack.170.place_ref, bf16[1024,512]{1,0:T(8,128)(2,1)S(1)} %add_convert_fusion.1.left_ref, bf16[512,896]{1,0:T(8,128)(2,1)S(1)} %get-tuple-element.44.right_ref, f32[64,896]{1,0:T(8,128)S(1)} %copy-done.1, f32[1,512]{1,0:T(1,128)S(1)} %bitcast.73), custom_call_target="tpu_custom_call" | custom-call | flops 939524096 | bytes 4194304 | tf_op jit(solution)/shard_map/pallas_call | solution.py:252
  (68 shorter events, 9.6 us)
Async XLA Ops:
  1.6 12.8 %collective-permute-start.3 = (bf16[64,896]{1,0:T(8,128)(2,1)S(1)}, bf16[64,896]{1,0:T(8,128)(2,1)S(1)}, u32[]{:S(2)}, u32[]{:S(2)}) collective-permute-start(bf16[64,896]{1,0:T(8,128)(2,1)S(1)} %convert_bitcast_fusion.refs_0_), channel_id=1, source_target_pairs={{0,128},{128,0},{1,129},{129,1},{2,130},{130,2},{3,131},{131,3},{4... | collective-permute-start | bytes 344072 | tf_op jit(solution)/shard_map/ppermute | solution.py:277
  9.4 6.8 %collective-permute-start.2 = (bf16[64,896]{1,0:T(8,128)(2,1)S(1)}, bf16[64,896]{1,0:T(8,128)(2,1)S(1)}, u32[]{:S(2)}, u32[]{:S(2)}) collective-permute-start(bf16[64,896]{1,0:T(8,128)(2,1)S(1)} %convert_bitcast_fusion.refs_0_), channel_id=1, source_target_pairs={{0,32},{32,64},{64,96},{96,0},{1,33},{33,65},{65,97},{97,1},{2,34}... | collective-permute-start | bytes 344072 | tf_op jit(solution)/shard_map/ppermute | solution.py:277
  10.7 10.4 %collective-permute-start.1 = (bf16[64,896]{1,0:T(8,128)(2,1)S(1)}, bf16[64,896]{1,0:T(8,128)(2,1)S(1)}, u32[]{:S(2)}, u32[]{:S(2)}) collective-permute-start(bf16[64,896]{1,0:T(8,128)(2,1)S(1)} %convert_bitcast_fusion.refs_0_), channel_id=1, source_target_pairs={{0,64},{32,96},{64,0},{96,32},{1,65},{33,97},{65,1},{97,33},{2,66}... | collective-permute-start | bytes 344072 | tf_op jit(solution)/shard_map/ppermute | solution.py:277
  13.3 7.8 %collective-permute-start = (bf16[64,896]{1,0:T(8,128)(2,1)S(1)}, bf16[64,896]{1,0:T(8,128)(2,1)S(1)}, u32[]{:S(2)}, u32[]{:S(2)}) collective-permute-start(bf16[64,896]{1,0:T(8,128)(2,1)S(1)} %convert_bitcast_fusion.refs_0_), channel_id=1, source_target_pairs={{0,96},{32,0},{64,32},{96,64},{1,97},{33,1},{65,33},{97,65},{2,98}... | collective-permute-start | bytes 344072 | tf_op jit(solution)/shard_map/ppermute | solution.py:277
  14.4 6.7 %collective-permute-start.6 = (bf16[64,896]{1,0:T(8,128)(2,1)S(1)}, bf16[64,896]{1,0:T(8,128)(2,1)S(1)}, u32[]{:S(2)}, u32[]{:S(2)}) collective-permute-start(bf16[64,896]{1,0:T(8,128)(2,1)S(1)} %collective-permute-done.3.refs_4_), channel_id=1, source_target_pairs={{0,32},{32,64},{64,96},{96,0},{1,33},{33,65},{65,97},{97,1},{2,34}... | collective-permute-start | bytes 344072 | tf_op jit(solution)/shard_map/ppermute | solution.py:277
  14.8 7.8 %collective-permute-start.5 = (bf16[64,896]{1,0:T(8,128)(2,1)S(1)}, bf16[64,896]{1,0:T(8,128)(2,1)S(1)}, u32[]{:S(2)}, u32[]{:S(2)}) collective-permute-start(bf16[64,896]{1,0:T(8,128)(2,1)S(1)} %collective-permute-done.3.refs_4_), channel_id=1, source_target_pairs={{0,64},{32,96},{64,0},{96,32},{1,65},{33,97},{65,1},{97,33},{2,66}... | collective-permute-start | bytes 344072 | tf_op jit(solution)/shard_map/ppermute | solution.py:277
  16.2 6.4 %collective-permute-start.4 = (bf16[64,896]{1,0:T(8,128)(2,1)S(1)}, bf16[64,896]{1,0:T(8,128)(2,1)S(1)}, u32[]{:S(2)}, u32[]{:S(2)}) collective-permute-start(bf16[64,896]{1,0:T(8,128)(2,1)S(1)} %collective-permute-done.3.refs_4_), channel_id=1, source_target_pairs={{0,96},{32,0},{64,32},{96,64},{1,97},{33,1},{65,33},{97,65},{2,98}... | collective-permute-start | bytes 344072 | tf_op jit(solution)/shard_map/ppermute | solution.py:277
  21.1 2.2 %copy-start.2 = (bf16[1024,896]{1,0:T(8,128)(2,1)S(1)}, bf16[1024,896]{1,0:T(8,128)(2,1)}, u32[]{:S(2)}) copy-start(bf16[1024,896]{1,0:T(8,128)(2,1)} %add_convert_fusion) | copy-start | bytes 5505028
  23.3 4.7 %copy-start.3 = (bf16[1024,896]{1,0:T(8,128)(2,1)S(1)}, bf16[1024,896]{1,0:T(8,128)(2,1)}, u32[]{:S(2)}) copy-start(bf16[1024,896]{1,0:T(8,128)(2,1)} %add_convert_fusion) | copy-start | bytes 5505028
  24.0 4.0 %collective-permute-start.7 = (bf16[512,512]{1,0:T(8,128)(2,1)S(1)}, bf16[512,512]{1,0:T(8,128)(2,1)}, u32[]{:S(2)}, u32[]{:S(2)}) collective-permute-start(bf16[512,512]{1,0:T(8,128)(2,1)S(1)} %convolution_convert_fusion.1), channel_id=1, source_target_pairs={{0,1},{1,0},{2,3},{3,2},{4,5},{5,4},{6,7},{7,6},{8,9},{9,8},{10,11... | collective-permute-start | bytes 1572872 | tf_op jit(solution)/shard_map/ppermute | solution.py:277
  29.8 5.1 %collective-permute-start.8 = (bf16[128,512]{1,0:T(8,128)(2,1)S(1)}, bf16[128,512]{1,0:T(8,128)(2,1)S(1)}, u32[]{:S(2)}, u32[]{:S(2)}) collective-permute-start(bf16[128,512]{1,0:T(8,128)(2,1)S(1)} %get-tuple-element.53), channel_id=1, source_target_pairs={{0,24},{8,0},{16,8},{24,16},{1,25},{9,1},{17,9},{25,17},{2,26},{10... | collective-permute-start | bytes 393224 | tf_op jit(solution)/shard_map/ppermute | solution.py:277
  32.4 6.9 %collective-permute-start.10 = (bf16[128,512]{1,0:T(8,128)(2,1)S(1)}, bf16[128,512]{1,0:T(8,128)(2,1)S(1)}, u32[]{:S(2)}, u32[]{:S(2)}) collective-permute-start(bf16[128,512]{1,0:T(8,128)(2,1)S(1)} %get-tuple-element.54), channel_id=1, source_target_pairs={{0,8},{8,16},{16,24},{24,0},{1,9},{9,17},{17,25},{25,1},{2,10},{10... | collective-permute-start | bytes 393224 | tf_op jit(solution)/shard_map/ppermute | solution.py:277
  32.4 7.5 %collective-permute-start.9 = (bf16[128,512]{1,0:T(8,128)(2,1)S(1)}, bf16[128,512]{1,0:T(8,128)(2,1)S(1)}, u32[]{:S(2)}, u32[]{:S(2)}) collective-permute-start(bf16[128,512]{1,0:T(8,128)(2,1)S(1)} %get-tuple-element.55), channel_id=1, source_target_pairs={{0,16},{8,24},{16,0},{24,8},{1,17},{9,25},{17,1},{25,9},{2,18},{10... | collective-permute-start | bytes 393224 | tf_op jit(solution)/shard_map/ppermute | solution.py:277
  40.0 4.7 %collective-permute-start.11 = (bf16[32,512]{1,0:T(8,128)(2,1)S(1)}, bf16[32,512]{1,0:T(8,128)(2,1)S(1)}, u32[]{:S(2)}, u32[]{:S(2)}) collective-permute-start(bf16[32,512]{1,0:T(8,128)(2,1)S(1)} %get-tuple-element.56), channel_id=1, source_target_pairs={{0,6},{2,0},{4,2},{6,4},{1,7},{3,1},{5,3},{7,5},{8,14},{10,8},{12,... | collective-permute-start | bytes 98312 | tf_op jit(solution)/shard_map/ppermute | solution.py:277
  42.1 4.6 %collective-permute-start.13 = (bf16[32,512]{1,0:T(8,128)(2,1)S(1)}, bf16[32,512]{1,0:T(8,128)(2,1)S(1)}, u32[]{:S(2)}, u32[]{:S(2)}) collective-permute-start(bf16[32,512]{1,0:T(8,128)(2,1)S(1)} %get-tuple-element.57), channel_id=1, source_target_pairs={{0,2},{2,4},{4,6},{6,0},{1,3},{3,5},{5,7},{7,1},{8,10},{10,12},{12... | collective-permute-start | bytes 98312 | tf_op jit(solution)/shard_map/ppermute | solution.py:277
  42.5 4.2 %collective-permute-start.12 = (bf16[32,512]{1,0:T(8,128)(2,1)S(1)}, bf16[32,512]{1,0:T(8,128)(2,1)S(1)}, u32[]{:S(2)}, u32[]{:S(2)}) collective-permute-start(bf16[32,512]{1,0:T(8,128)(2,1)S(1)} %get-tuple-element.58), channel_id=1, source_target_pairs={{0,4},{2,6},{4,0},{6,2},{1,5},{3,7},{5,1},{7,3},{8,12},{10,14},{12... | collective-permute-start | bytes 98312 | tf_op jit(solution)/shard_map/ppermute | solution.py:277
  67.3 3.7 %collective-permute-start.14 = (bf16[512,512]{1,0:T(8,128)(2,1)S(1)}, bf16[512,512]{1,0:T(8,128)(2,1)S(1)}, u32[]{:S(2)}, u32[]{:S(2)}) collective-permute-start(bf16[512,512]{1,0:T(8,128)(2,1)S(1)} %bitcast.70), channel_id=1, source_target_pairs={{0,1},{1,0},{2,3},{3,2},{4,5},{5,4},{6,7},{7,6},{8,9},{9,8},{10,11... | collective-permute-start | bytes 1572872 | tf_op jit(solution)/shard_map/ppermute | solution.py:277
  72.4 17.2 %all-to-all-start.1 = ((f32[8,40,128]{2,1,0:T(8,128)}), f32[8,40,128]{2,1,0:T(8,128)S(1)}, u32[]{:S(2)}, u32[]{:S(2)}) async-start(f32[8,40,128]{2,1,0:T(8,128)} %broadcast_in_dim.11), calls=%async_computation.1 | async-start | bytes 327680 | tf_op jit(solution)/shard_map/all_to_all | solution.py:272
  83.5 10.1 %collective-permute-start.17 = (bf16[128,896]{1,0:T(8,128)(2,1)S(1)}, bf16[128,896]{1,0:T(8,128)(2,1)S(1)}, u32[]{:S(2)}, u32[]{:S(2)}) collective-permute-start(bf16[128,896]{1,0:T(8,128)(2,1)S(1)} %get-tuple-element.49), channel_id=1, source_target_pairs={{0,32},{32,64},{64,96},{96,0},{1,33},{33,65},{65,97},{97,1},{2,34}... | collective-permute-start | bytes 688136 | tf_op jit(solution)/shard_map/ppermute | solution.py:277
  85.0 13.3 %collective-permute-start.16 = (bf16[128,896]{1,0:T(8,128)(2,1)S(1)}, bf16[128,896]{1,0:T(8,128)(2,1)S(1)}, u32[]{:S(2)}, u32[]{:S(2)}) collective-permute-start(bf16[128,896]{1,0:T(8,128)(2,1)S(1)} %get-tuple-element.50), channel_id=1, source_target_pairs={{0,64},{32,96},{64,0},{96,32},{1,65},{33,97},{65,1},{97,33},{2,66}... | collective-permute-start | bytes 688136 | tf_op jit(solution)/shard_map/ppermute | solution.py:277
  87.4 10.9 %collective-permute-start.15 = (bf16[128,896]{1,0:T(8,128)(2,1)S(1)}, bf16[128,896]{1,0:T(8,128)(2,1)S(1)}, u32[]{:S(2)}, u32[]{:S(2)}) collective-permute-start(bf16[128,896]{1,0:T(8,128)(2,1)S(1)} %get-tuple-element.51), channel_id=1, source_target_pairs={{0,96},{32,0},{64,32},{96,64},{1,97},{33,1},{65,33},{97,65},{2,98}... | collective-permute-start | bytes 688136 | tf_op jit(solution)/shard_map/ppermute | solution.py:277
  90.2 8.2 %all-to-all-start.2 = ((f32[4,40,128]{2,1,0:T(8,128)}), f32[4,40,128]{2,1,0:T(8,128)S(1)}, u32[]{:S(2)}, u32[]{:S(2)}) async-start(f32[4,40,128]{2,1,0:T(8,128)} %broadcast_in_dim.12), calls=%async_computation.2 | async-start | bytes 163840 | tf_op jit(solution)/shard_map/all_to_all | solution.py:272
  98.6 11.7 %collective-permute-start.18 = (bf16[128,896]{1,0:T(8,128)(2,1)S(1)}, bf16[128,896]{1,0:T(8,128)(2,1)S(1)}, u32[]{:S(2)}, u32[]{:S(2)}) collective-permute-start(bf16[128,896]{1,0:T(8,128)(2,1)S(1)} %add_convert_fusion.3), channel_id=1, source_target_pairs={{0,128},{128,0},{1,129},{129,1},{2,130},{130,2},{3,131},{131,3},{4... | collective-permute-start | bytes 688136 | tf_op jit(solution)/shard_map/ppermute | solution.py:277
  102.7 5.4 %collective-permute-start.21 = (f32[160,128]{1,0:T(8,128)S(1)}, f32[160,128]{1,0:T(8,128)S(1)}, u32[]{:S(2)}, u32[]{:S(2)}) collective-permute-start(f32[160,128]{1,0:T(8,128)S(1)} %bitcast.74), channel_id=1, source_target_pairs={{0,8},{8,16},{16,24},{24,0},{1,9},{9,17},{17,25},{25,1},{2,10},{10... | collective-permute-start | bytes 245768 | tf_op jit(solution)/shard_map/ppermute | solution.py:277
  102.7 5.4 %collective-permute-start.20 = (f32[160,128]{1,0:T(8,128)S(1)}, f32[160,128]{1,0:T(8,128)S(1)}, u32[]{:S(2)}, u32[]{:S(2)}) collective-permute-start(f32[160,128]{1,0:T(8,128)S(1)} %bitcast.75), channel_id=1, source_target_pairs={{0,16},{8,24},{16,0},{24,8},{1,17},{9,25},{17,1},{25,9},{2,18},{10... | collective-permute-start | bytes 245768 | tf_op jit(solution)/shard_map/ppermute | solution.py:277
  104.5 4.2 %collective-permute-start.19 = (f32[160,128]{1,0:T(8,128)S(1)}, f32[160,128]{1,0:T(8,128)S(1)}, u32[]{:S(2)}, u32[]{:S(2)}) collective-permute-start(f32[160,128]{1,0:T(8,128)S(1)} %bitcast.76), channel_id=1, source_target_pairs={{0,24},{8,0},{16,8},{24,16},{1,25},{9,1},{17,9},{25,17},{2,26},{10... | collective-permute-start | bytes 245768 | tf_op jit(solution)/shard_map/ppermute | solution.py:277
  110.3 4.3 %collective-permute-start.22 = (f32[640,128]{1,0:T(8,128)S(1)}, f32[640,128]{1,0:T(8,128)S(1)}, u32[]{:S(2)}, u32[]{:S(2)}) collective-permute-start(f32[640,128]{1,0:T(8,128)S(1)} %constant_dynamic-update-slice_fusion.own_ref), channel_id=1, source_target_pairs={{0,1},{1,0},{2,3},{3,2},{4,5},{5,4},{6,7},{7,6},{8,9},{9,8},{10,11... | collective-permute-start | bytes 983048 | tf_op jit(solution)/shard_map/ppermute | solution.py:277
  114.7 24.2 %collective-permute-start.25 = (bf16[128,896]{1,0:T(8,128)(2,1)S(1)}, bf16[128,896]{1,0:T(8,128)(2,1)S(1)}, u32[]{:S(2)}, u32[]{:S(2)}) collective-permute-start(bf16[128,896]{1,0:T(8,128)(2,1)S(1)} %add_convert_fusion.2.refs_0_), channel_id=1, source_target_pairs={{0,32},{32,64},{64,96},{96,0},{1,33},{33,65},{65,97},{97,1},{2,34}... | collective-permute-start | bytes 688136 | tf_op jit(solution)/shard_map/ppermute | solution.py:277
  117.9 21.0 %collective-permute-start.24 = (bf16[128,896]{1,0:T(8,128)(2,1)S(1)}, bf16[128,896]{1,0:T(8,128)(2,1)S(1)}, u32[]{:S(2)}, u32[]{:S(2)}) collective-permute-start(bf16[128,896]{1,0:T(8,128)(2,1)S(1)} %add_convert_fusion.2.refs_0_), channel_id=1, source_target_pairs={{0,64},{32,96},{64,0},{96,32},{1,65},{33,97},{65,1},{97,33},{2,66}... | collective-permute-start | bytes 688136 | tf_op jit(solution)/shard_map/ppermute | solution.py:277
  120.4 18.5 %collective-permute-start.23 = (bf16[128,896]{1,0:T(8,128)(2,1)S(1)}, bf16[128,896]{1,0:T(8,128)(2,1)S(1)}, u32[]{:S(2)}, u32[]{:S(2)}) collective-permute-start(bf16[128,896]{1,0:T(8,128)(2,1)S(1)} %add_convert_fusion.2.refs_0_), channel_id=1, source_target_pairs={{0,96},{32,0},{64,32},{96,64},{1,97},{33,1},{65,33},{97,65},{2,98}... | collective-permute-start | bytes 688136 | tf_op jit(solution)/shard_map/ppermute | solution.py:277
  140.8 0.7 copy-start
  142.2 13.3 %all-to-all-start.3 = ((f32[32,1,512]{2,1,0:T(1,128)}), f32[32,1,512]{2,1,0:T(1,128)}, u32[]{:S(2)}, u32[]{:S(2)}) async-start(f32[32,1,512]{2,1,0:T(1,128)} %broadcast_in_dim.14), calls=%async_computation.3 | async-start | bytes 131072 | tf_op jit(solution)/shard_map/all_to_all | solution.py:272
  148.3 1.5 copy-start.4
  149.8 6.6 %copy-start.1 = (f32[64,896]{1,0:T(8,128)S(1)}, f32[64,896]{1,0:T(8,128)}, u32[]{:S(2)}) copy-start(f32[64,896]{1,0:T(8,128)} %copy-done) | copy-start | bytes 688132
where the time goes:
time: 161 us; the launch traced here: 160 us
  starting transfers between devices  66.3 us (41%)
  waiting for transfers between devices  26.9 us (17%)
  Pallas kernels  25.1 us (16%)
  blocking collectives  20.5 us (13%)
  matrix products  10.2 us (6%)
  other arithmetic  5.96 us (4%)
  local copies, waits for them, and re-layouts  4.04 us (3%)
    ppermute x26, starting transfers between devices, from_ahead(): lax.ppermute(value, axis, [(i, (i - steps) % length) for i in range(lengt...  50.1 us
    ppermute x26, waiting for transfers between devices, from_ahead(): lax.ppermute(value, axis, [(i, (i - steps) % length) for i in range(lengt...  22.5 us
    pallas_call x4, Pallas kernels, kernel_call(): pl.pallas_call(kernel, out_shape=outputs, in_specs=[pl.BlockSpec(memory_s...  21.5 us
    all_to_all x1, blocking collectives, from_everyone(): lax.all_to_all(jnp.broadcast_to(value[None], (length, *value.shape)), axi...  20.5 us
    all_to_all x3, starting transfers between devices, from_everyone(): lax.all_to_all(jnp.broadcast_to(value[None], (length, *value.shape)), axi...  16.2 us
    dot_general x8, matrix products, product(): lax.dot_general(left, right, (((left_dim,), (right_dim,)), ((), ())), pre...  10.2 us
    all_to_all x3, waiting for transfers between devices, from_everyone(): lax.all_to_all(jnp.broadcast_to(value[None], (length, *value.shape)), axi...  4.31 us
    convert_element_type x1, other arithmetic, on_device(): blended = (momentum.astype(f32) + gradient.astype(f32)).astype(bf16)  3.73 us
  transfers between devices with their start and end apart: 29, of which 15 were waited for; matrix products, arithmetic and copies ran while one was open for 8% of the time, Pallas kernels for 12%

commit v1 on v0

--- a/solution.py
+++ b/solution.py
@@ -208,7 +208,8 @@
         right_ref[band, :] = right.astype(bf16)
         square = right * right
         folded = added([square[:, at : at + BLOCK] for at in range(0, right.shape[1], BLOCK)])
-        sums_ref[:, band] = jnp.sum(folded.T, axis=0, keepdims=True)
+        row = jnp.sum(folded.T, axis=0, keepdims=True)
+        sums_ref[:, :, band] = jnp.broadcast_to(row[None], (2 * FAR, 1, BLOCK))
     rows = own_ref.shape[0]
     own_ref[...] = whole[pl.ds(pl.multiple_of(place_ref[4] * rows, rows), rows), :]
 
@@ -222,49 +223,48 @@
         [
             jax.ShapeDtypeStruct((R, width), bf16),
             jax.ShapeDtypeStruct((rows, width), f32),
-            jax.ShapeDtypeStruct((1, R), f32),
+            jax.ShapeDtypeStruct((2 * FAR, 1, R), f32),
         ],
         [((R, width), bf16), ((R, width), f32)],
         4 * R * R * width,
     )
 
 
-def update_kernel(place_ref, left_ref, right_ref, own_ref, inverse_ref, update_ref, factor_ref, column):
-    @pl.when(pl.program_id(0) == 0)
+def update_kernel(place_ref, left_ref, right_ref, own_ref, sums_ref, update_ref, factor_ref, inverse, column):
+    step = pl.program_id(0)
+
+    @pl.when(step == 0)
     def _():
+        inverse[...] = lax.rsqrt(jnp.sum(sums_ref[...], axis=0) + epsilon)
+        column[...] = jnp.broadcast_to(inverse[...], (BLOCK, R)).T
         rows = own_ref.shape[0]
-        column[...] = jnp.broadcast_to(inverse_ref[...], (BLOCK, R)).T
         scale = column[pl.ds(pl.multiple_of(place_ref[4] * rows, rows), rows), :]
         for at in range(0, own_ref.shape[1], BLOCK):
             factor_ref[:, at : at + BLOCK] = own_ref[:, at : at + BLOCK] * scale
 
-    scaled = (left_ref[...].astype(f32) * inverse_ref[...]).astype(bf16)
+    band = update_ref.shape[0]
+    left = left_ref[pl.ds(pl.multiple_of(step * band, band), band), :]
+    scaled = (left.astype(f32) * inverse[...]).astype(bf16)
     update_ref[...] = (product(scaled, right_ref[...], 1, 0) * math.sqrt(D * FF / R)).astype(bf16)
 
 
-def update_side(place, left, right, own, inverse):
+def update_side(place, left, right, own, sums):
     height, width = left.shape[0], right.shape[1]
-    band = height // 4
-
-    def fixed(value):
-        return pl.BlockSpec(value.shape, lambda i: (0, 0))
-
+    steps = 4
+    whole = pl.BlockSpec(memory_space=pltpu.VMEM)
     return pl.pallas_call(
         update_kernel,
-        grid=(4,),
+        grid=(steps,),
         out_shape=[jax.ShapeDtypeStruct((height, width), bf16), jax.ShapeDtypeStruct(own.shape, f32)],
-        in_specs=[
-            pl.BlockSpec(memory_space=pltpu.SMEM),
-            pl.BlockSpec((band, R), lambda i: (i, 0)),
-            fixed(right),
-            fixed(own),
-            fixed(inverse),
+        in_specs=[pl.BlockSpec(memory_space=pltpu.SMEM)] + [whole] * 4,
+        out_specs=[
+            pl.BlockSpec((height // steps, width), lambda i: (i, 0)),
+            pl.BlockSpec(own.shape, lambda i: (0, 0)),
         ],
-        out_specs=[pl.BlockSpec((band, width), lambda i: (i, 0)), fixed(own)],
-        scratch_shapes=[pltpu.VMEM((R, BLOCK), f32)],
+        scratch_shapes=[pltpu.VMEM((1, R), f32), pltpu.VMEM((R, BLOCK), f32)],
         compiler_params=pltpu.CompilerParams(vmem_limit_bytes=12 << 20),
         cost_estimate=pl.CostEstimate(flops=2 * R * height * width, bytes_accessed=4 << 20, transcendentals=0),
-    )(place, left, right, own, inverse)
+    )(place, left, right, own, sums)
 
 
 def from_everyone(value, axis):
@@ -314,7 +314,8 @@
 
     sent = product(other_rows, all_lowered, 1, 1).astype(bf16)
     arrived = from_ahead(sent, "core", 1)
-    partial_left = (product(own_rows, all_lowered, 1, 1) + arrived.astype(f32)).astype(bf16)
+    kept = lax.optimization_barrier(product(own_rows, all_lowered, 1, 1))
+    partial_left = (kept + arrived.astype(f32)).astype(bf16)
     left_line = total(exchanged(partial_left, "x", x)).astype(bf16)
     left_rows = total(exchanged(left_line, "z_lo", z_lo)).astype(bf16)
     own_left = from_everyone(left_rows, ("x", "z_lo")).reshape(half, R)
@@ -345,13 +346,12 @@
     high, low = inverse_factor(gram_place, own_gram, other_gram)
     right_factor, own_right, own_sums = right_side(right_place, high, low, right_pieces, columns)
 
-    last_left, own_sums = lax.optimization_barrier((left_factor, own_sums))
-    square_sums = jnp.sum(from_everyone(own_sums, TENSOR), axis=(0, 1))
+    last_left = left_factor
+    sums = lax.all_to_all(own_sums, TENSOR, 0, 0, tiled=True)
     orthonormal = (product(last_left, high, 1, 1) + product(last_left, low, 1, 1)).astype(bf16)
     taken = product(orthonormal, right_factor, 1, 0)
     new_momentum = (blended.astype(f32) - (1.0 - decay_rate) * taken).astype(bf16)
-    inverse = lax.rsqrt(square_sums + epsilon)[None]
-    update, own_factor = update_side(right_place, orthonormal, right_factor, own_right, inverse)
+    update, own_factor = update_side(right_place, orthonormal, right_factor, own_right, sums)
     return (new_momentum, own_factor.T, update)
 
 

time: 161 us -> 159 us (0.988)
  starting transfers between devices: 66.3 us -> 58.1 us
  waiting for transfers between devices: 26.9 us -> 32.5 us
  local copies, waits for them, and re-layouts: 4.04 us -> 1.94 us
    all_to_all x3 -> x2, starting transfers between devices: 16.2 us -> 9.45 us  [from_everyone(): lax.all_to_all(jnp.broadcast_to(value[None], (length, *value.shape)), axi...]
    ppermute x26, starting transfers between devices: 50.1 us -> 44.2 us  [from_ahead(): lax.ppermute(value, axis, [(i, (i - steps) % length) for i in range(lengt...]
    all_to_all x0 -> x1, starting transfers between devices: none -> 4.44 us  [on_device(): sums = lax.all_to_all(own_sums, TENSOR, 0, 0, tiled=True)]
    ppermute x26, waiting for transfers between devices: 22.5 us -> 26.5 us  [from_ahead(): lax.ppermute(value, axis, [(i, (i - steps) % length) for i in range(lengt...]
    all_to_all x0 -> x1, waiting for transfers between devices: none -> 3.88 us  [on_device(): sums = lax.all_to_all(own_sums, TENSOR, 0, 0, tiled=True)]
    all_to_all x3 -> x2, waiting for transfers between devices: 4.31 us -> 2.12 us  [from_everyone(): lax.all_to_all(jnp.broadcast_to(value[None], (length, *value.shape)), axi...]
    dot_general x8, matrix products: 10.2 us -> 11.8 us  [product(): lax.dot_general(left, right, (((left_dim,), (right_dim,)), ((), ())), pre...]
  transfers between devices with their start and end apart: 29 -> 29, of which waited for: 15 -> 18; matrix products, arithmetic and copies ran while one was open for 8% -> 10% of each run, Pallas kernels for 12% -> 12%
where the time goes in v1:
time: 159 us; the launch traced here: 158 us
  starting transfers between devices  58.1 us (37%)
  waiting for transfers between devices  32.5 us (20%)
  Pallas kernels  25.9 us (16%)
  blocking collectives  21.7 us (14%)
  matrix products  11.8 us (7%)
  other arithmetic  5.21 us (3%)
  local copies, waits for them, and re-layouts  1.94 us (1%)
    ppermute x26, starting transfers between devices, from_ahead(): lax.ppermute(value, axis, [(i, (i - steps) % length) for i in range(lengt...  44.2 us
    ppermute x26, waiting for transfers between devices, from_ahead(): lax.ppermute(value, axis, [(i, (i - steps) % length) for i in range(lengt...  26.5 us
    pallas_call x4, Pallas kernels, kernel_call(): pl.pallas_call(kernel, out_shape=outputs, in_specs=[pl.BlockSpec(memory_s...  22.2 us
    all_to_all x1, blocking collectives, from_everyone(): lax.all_to_all(jnp.broadcast_to(value[None], (length, *value.shape)), axi...  21.7 us
    dot_general x8, matrix products, product(): lax.dot_general(left, right, (((left_dim,), (right_dim,)), ((), ())), pre...  11.8 us
    all_to_all x2, starting transfers between devices, from_everyone(): lax.all_to_all(jnp.broadcast_to(value[None], (length, *value.shape)), axi...  9.45 us
    all_to_all x1, starting transfers between devices, on_device(): sums = lax.all_to_all(own_sums, TENSOR, 0, 0, tiled=True)  4.44 us
    all_to_all x1, waiting for transfers between devices, on_device(): sums = lax.all_to_all(own_sums, TENSOR, 0, 0, tiled=True)  3.88 us
  transfers between devices with their start and end apart: 29, of which 18 were waited for; matrix products, arithmetic and copies ran while one was open for 10% of the time, Pallas kernels for 12%

profile of v1, /device:TPU:1, one launch (start us, length us, event | category | flops | bytes accessed | tf_op | source)
XLA Modules:
  0.0 158.2 jit_solution(2409594598869090983)
XLA Ops:
  0.6 1.0 convert_bitcast_fusion.refs_0_
  1.6 7.8 %collective-permute-start.3 = (bf16[64,896]{1,0:T(8,128)(2,1)S(1)}, bf16[64,896]{1,0:T(8,128)(2,1)S(1)}, u32[]{:S(2)}, u32[]{:S(2)}) collective-permute-start(bf16[64,896]{1,0:T(8,128)(2,1)S(1)} %convert_bitcast_fusion.refs_0_), channel_id=1, source_target_pairs={{0,128},{128,0},{1,129},{129,1},{2,130},{130,2},{3,131},{131,3},{4... | collective-permute-start | bytes 344072 | tf_op jit(solution)/shard_map/ppermute | solution.py:277
  9.4 2.7 %collective-permute-start = (bf16[64,896]{1,0:T(8,128)(2,1)S(1)}, bf16[64,896]{1,0:T(8,128)(2,1)S(1)}, u32[]{:S(2)}, u32[]{:S(2)}) collective-permute-start(bf16[64,896]{1,0:T(8,128)(2,1)S(1)} %convert_bitcast_fusion.refs_0_), channel_id=1, source_target_pairs={{0,96},{32,0},{64,32},{96,64},{1,97},{33,1},{65,33},{97,65},{2,98}... | collective-permute-start | bytes 344072 | tf_op jit(solution)/shard_map/ppermute | solution.py:277
  12.5 0.7 collective-permute-start.2
  13.2 2.0 %collective-permute-start.4 = (bf16[64,896]{1,0:T(8,128)(2,1)S(1)}, bf16[64,896]{1,0:T(8,128)(2,1)S(1)}, u32[]{:S(2)}, u32[]{:S(2)}) collective-permute-start(bf16[64,896]{1,0:T(8,128)(2,1)S(1)} %collective-permute-done.3.refs_4_), channel_id=1, source_target_pairs={{0,96},{32,0},{64,32},{96,64},{1,97},{33,1},{65,33},{97,65},{2,98}... | collective-permute-start | bytes 344072 | tf_op jit(solution)/shard_map/ppermute | solution.py:277
  15.2 1.4 collective-permute-start.5
  16.6 3.7 %add_convert_fusion = bf16[1024,896]{1,0:T(8,128)(2,1)} fusion(bf16[1024,896]{1,0:T(8,128)(2,1)} %param.4, bf16[1024,896]{1,0:T(8,128)(2,1)} %param.3), kind=kLoop, calls=%fused_computation.1 | loop fusion | flops 3670016 | bytes 5505024 | tf_op jit(solution)/shard_map/convert_element_type | solution.py:310
  20.4 1.1 collective-permute-done.2.refs_3_
  21.7 2.8 %collective-permute-done.6.refs_7_ = bf16[64,896]{1,0:T(8,128)(2,1)S(1)} collective-permute-done((bf16[64,896]{1,0:T(8,128)(2,1)S(1)}, bf16[64,896]{1,0:T(8,128)(2,1)S(1)}, u32[]{:S(2)}, u32[]{:S(2)}) %collective-permute-start.6) | collective-permute-done | bytes 114720 | tf_op jit(solution)/shard_map/ppermute | solution.py:277
  25.1 0.7 convolution_convert_fusion.1
  25.8 2.2 %collective-permute-start.7 = (bf16[512,512]{1,0:T(8,128)(2,1)S(1)}, bf16[512,512]{1,0:T(8,128)(2,1)S(1)}, u32[]{:S(2)}, u32[]{:S(2)}) collective-permute-start(bf16[512,512]{1,0:T(8,128)(2,1)S(1)} %convolution_convert_fusion.1), channel_id=1, source_target_pairs={{0,1},{1,0},{2,3},{3,2},{4,5},{5,4},{6,7},{7,6},{8,9},{9,8},{10,11... | collective-permute-start | bytes 1572872 | tf_op jit(solution)/shard_map/ppermute | solution.py:277
  28.1 1.9 %fusion.1 = f32[512,512]{1,0:T(8,128)S(1)} fusion(bf16[512,896]{1,0:T(8,128)(2,1)S(1)} %shard_map.58, bf16[1024,896]{1,0:T(8,128)(2,1)} %add_convert_fusion, s32[]{:T(128)S(6)} %select_n.272), kind=kOutput, calls=%fused_computation.9 | convolution fusion | flops 469762048 | bytes 2883588 | tf_op jit(solution)/shard_map/dot_general | solution.py:29
  30.2 1.3 collective-permute-start.10
  31.5 2.5 %collective-permute-start.9 = (bf16[128,512]{1,0:T(8,128)(2,1)S(1)}, bf16[128,512]{1,0:T(8,128)(2,1)S(1)}, u32[]{:S(2)}, u32[]{:S(2)}) collective-permute-start(bf16[128,512]{1,0:T(8,128)(2,1)S(1)} %get-tuple-element.51), channel_id=1, source_target_pairs={{0,16},{8,24},{16,0},{24,8},{1,17},{9,25},{17,1},{25,9},{2,18},{10... | collective-permute-start | bytes 393224 | tf_op jit(solution)/shard_map/ppermute | solution.py:277
  33.9 1.2 collective-permute-start.8
  35.1 1.4 collective-permute-done.10
  36.5 3.8 %collective-permute-done.9 = bf16[128,512]{1,0:T(8,128)(2,1)S(1)} collective-permute-done((bf16[128,512]{1,0:T(8,128)(2,1)S(1)}, bf16[128,512]{1,0:T(8,128)(2,1)S(1)}, u32[]{:S(2)}, u32[]{:S(2)}) %collective-permute-start.9) | collective-permute-done | bytes 131104 | tf_op jit(solution)/shard_map/ppermute | solution.py:277
  40.4 0.8 collective-permute-start.13
  41.3 1.3 collective-permute-start.12
  42.6 2.3 %collective-permute-start.11 = (bf16[32,512]{1,0:T(8,128)(2,1)S(1)}, bf16[32,512]{1,0:T(8,128)(2,1)S(1)}, u32[]{:S(2)}, u32[]{:S(2)}) collective-permute-start(bf16[32,512]{1,0:T(8,128)(2,1)S(1)} %get-tuple-element.52), channel_id=1, source_target_pairs={{0,6},{2,0},{4,2},{6,4},{1,7},{3,1},{5,3},{7,5},{8,14},{10,8},{12,... | collective-permute-start | bytes 98312 | tf_op jit(solution)/shard_map/ppermute | solution.py:277
  45.9 21.7 %all_to_all.20 = bf16[16,32,512]{2,1,0:T(8,128)(2,1)S(1)} all-to-all(bf16[16,32,512]{2,1,0:T(8,128)(2,1)S(1)} %broadcast_in_dim.6), channel_id=1, replica_groups=mesh['z_hi'=2,'y'=4,'x'=4,'z_lo'=4,'core'=2] {'x','z_lo'}, dimensions={0} | all-to-all | bytes 1048576 | tf_op jit(solution)/shard_map/all_to_all | solution.py:272
  67.6 2.4 %collective-permute-start.14 = (bf16[512,512]{1,0:T(8,128)(2,1)S(1)}, bf16[512,512]{1,0:T(8,128)(2,1)S(1)}, u32[]{:S(2)}, u32[]{:S(2)}) collective-permute-start(bf16[512,512]{1,0:T(8,128)(2,1)S(1)} %bitcast.68), channel_id=1, source_target_pairs={{0,1},{1,0},{2,3},{3,2},{4,5},{5,4},{6,7},{7,6},{8,9},{9,8},{10,11... | collective-permute-start | bytes 1572872 | tf_op jit(solution)/shard_map/ppermute | solution.py:277
  70.5 1.0 collective-permute-done.14.refs_1_
  72.2 0.7 broadcast_in_dim.7
  72.9 6.2 %all-to-all-start.1 = ((f32[8,40,128]{2,1,0:T(8,128)}), f32[8,40,128]{2,1,0:T(8,128)S(1)}, u32[]{:S(2)}, u32[]{:S(2)}) async-start(f32[8,40,128]{2,1,0:T(8,128)} %broadcast_in_dim.7), calls=%async_computation.1 | async-start | bytes 327680 | tf_op jit(solution)/shard_map/all_to_all | solution.py:272
  79.6 2.8 %convolution_convert_fusion = bf16[512,896]{1,0:T(8,128)(2,1)S(1)} fusion(bf16[1024,512]{1,0:T(8,128)(2,1)S(1)} %shard_map.59, bf16[1024,896]{1,0:T(8,128)(2,1)} %add_convert_fusion), kind=kOutput, calls=%fused_computation.3 | convolution fusion | flops 939982848 | bytes 3801088 | tf_op jit(solution)/shard_map/dot_general | solution.py:29
  82.5 2.8 %collective-permute-start.15 = (bf16[128,896]{1,0:T(8,128)(2,1)S(1)}, bf16[128,896]{1,0:T(8,128)(2,1)S(1)}, u32[]{:S(2)}, u32[]{:S(2)}) collective-permute-start(bf16[128,896]{1,0:T(8,128)(2,1)S(1)} %get-tuple-element.47), channel_id=1, source_target_pairs={{0,96},{32,0},{64,32},{96,64},{1,97},{33,1},{65,33},{97,65},{2,98}... | collective-permute-start | bytes 688136 | tf_op jit(solution)/shard_map/ppermute | solution.py:277
  86.4 2.1 %all-to-all-done.1 = f32[8,40,128]{2,1,0:T(8,128)S(1)} async-done(((f32[8,40,128]{2,1,0:T(8,128)}), f32[8,40,128]{2,1,0:T(8,128)S(1)}, u32[]{:S(2)}, u32[]{:S(2)}) %all-to-all-start.1) | async-done | bytes 163872 | tf_op jit(solution)/shard_map/all_to_all | solution.py:272
  88.6 0.6 broadcast_in_dim.8
  89.2 3.3 %all-to-all-start.2 = ((f32[4,40,128]{2,1,0:T(8,128)}), f32[4,40,128]{2,1,0:T(8,128)S(1)}, u32[]{:S(2)}, u32[]{:S(2)}) async-start(f32[4,40,128]{2,1,0:T(8,128)} %broadcast_in_dim.8), calls=%async_computation.2 | async-start | bytes 163840 | tf_op jit(solution)/shard_map/all_to_all | solution.py:272
  92.5 1.1 collective-permute-done.16
  93.6 6.1 %collective-permute-done.17 = bf16[128,896]{1,0:T(8,128)(2,1)S(1)} collective-permute-done((bf16[128,896]{1,0:T(8,128)(2,1)S(1)}, bf16[128,896]{1,0:T(8,128)(2,1)S(1)}, u32[]{:S(2)}, u32[]{:S(2)}) %collective-permute-start.17) | collective-permute-done | bytes 229408 | tf_op jit(solution)/shard_map/ppermute | solution.py:277
  99.8 4.7 %collective-permute-start.18 = (bf16[128,896]{1,0:T(8,128)(2,1)S(1)}, bf16[128,896]{1,0:T(8,128)(2,1)S(1)}, u32[]{:S(2)}, u32[]{:S(2)}) collective-permute-start(bf16[128,896]{1,0:T(8,128)(2,1)S(1)} %add_convert_fusion.4), channel_id=1, source_target_pairs={{0,128},{128,0},{1,129},{129,1},{2,130},{130,2},{3,131},{131,3},{4... | collective-permute-start | bytes 688136 | tf_op jit(solution)/shard_map/ppermute | solution.py:277
  106.0 2.1 %collective-permute-done.19 = f32[160,128]{1,0:T(8,128)S(1)} collective-permute-done((f32[160,128]{1,0:T(8,128)S(1)}, f32[160,128]{1,0:T(8,128)S(1)}, u32[]{:S(2)}, u32[]{:S(2)}) %collective-permute-start.19) | collective-permute-done | bytes 81952 | tf_op jit(solution)/shard_map/ppermute | solution.py:277
  108.1 2.1 %collective-permute-done.20 = f32[160,128]{1,0:T(8,128)S(1)} collective-permute-done((f32[160,128]{1,0:T(8,128)S(1)}, f32[160,128]{1,0:T(8,128)S(1)}, u32[]{:S(2)}, u32[]{:S(2)}) %collective-permute-start.20) | collective-permute-done | bytes 81952 | tf_op jit(solution)/shard_map/ppermute | solution.py:277
  110.2 1.1 collective-permute-done.21
  111.3 1.8 %collective-permute-done.18 = bf16[128,896]{1,0:T(8,128)(2,1)S(1)} collective-permute-done((bf16[128,896]{1,0:T(8,128)(2,1)S(1)}, bf16[128,896]{1,0:T(8,128)(2,1)S(1)}, u32[]{:S(2)}, u32[]{:S(2)}) %collective-permute-start.18) | collective-permute-done | bytes 229408 | tf_op jit(solution)/shard_map/ppermute | solution.py:277
  113.2 3.7 %collective-permute-start.22 = (f32[640,128]{1,0:T(8,128)S(1)}, f32[640,128]{1,0:T(8,128)S(1)}, u32[]{:S(2)}, u32[]{:S(2)}) collective-permute-start(f32[640,128]{1,0:T(8,128)S(1)} %constant_dynamic-update-slice_fusion.own_ref), channel_id=1, source_target_pairs={{0,1},{1,0},{2,3},{3,2},{4,5},{5,4},{6,7},{7,6},{8,9},{9,8},{10,11... | collective-permute-start | bytes 983048 | tf_op jit(solution)/shard_map/ppermute | solution.py:277
  117.2 1.0 collective-permute-done.22.other_ref
  118.2 1.5 collective-permute-start.25
  119.6 18.3 %shard_map.60 = (bf16[512,512]{1,0:T(8,128)(2,1)S(1)}, bf16[512,512]{1,0:T(8,128)(2,1)S(1)}) custom-call(s32[32]{0:T(128)S(1)} %stack.197.place_ref, f32[640,128]{1,0:T(8,128)S(1)} %constant_dynamic-update-slice_fusion.own_ref, f32[640,128]{1,0:T(8,128)S(1)} %collective-permute-done.22.other_ref), custom_call_target="tpu_custom_call" | custom-call | flops 2684354560 | bytes 2097152 | tf_op jit(solution)/shard_map/pallas_call | solution.py:162
  137.9 0.7 fusion.5
  138.7 0.7 add_convert_fusion.1.left_ref
  139.5 2.7 %shard_map.61 = (bf16[512,896]{1,0:T(8,128)(2,1)S(1)}, f32[64,896]{1,0:T(8,128)S(1)}, f32[32,1,512]{2,1,0:T(1,128)}) custom-call(s32[5]{0:T(128)S(1)} %stack.203.place_ref, bf16[512,512]{1,0:T(8,128)(2,1)S(1)} %get-tuple-element.37.high_ref, bf16[512,512]{1,0:T(8,128)(2,1)S(1)} %get-tuple-element.38.low_ref, bf16[128,896]{1,0:T(8,128)(2,1)S(1)} %add_convert_fusion.3.refs_0_, ...), custom_call_target="tpu_custom_call" | custom-call | flops 939524096 | bytes 2097152 | tf_op jit(solution)/shard_map/pallas_call | solution.py:162
  142.1 4.4 %all-to-all-start.3 = ((f32[32,1,512]{2,1,0:T(1,128)}), f32[32,1,512]{2,1,0:T(1,128)S(1)}, u32[]{:S(2)}, u32[]{:S(2)}) async-start(f32[32,1,512]{2,1,0:T(1,128)} %get-tuple-element.42), calls=%async_computation.3 | async-start | bytes 131072 | tf_op jit(solution)/shard_map/all_to_all | solution.py:350
  146.6 4.0 %subtract_convert_fusion = bf16[1024,896]{1,0:T(8,128)(2,1)} fusion(bf16[1024,896]{1,0:T(8,128)(2,1)} %add_convert_fusion, bf16[1024,512]{1,0:T(8,128)(2,1)S(1)} %add_convert_fusion.1.left_ref, bf16[512,896]{1,0:T(8,128)(2,1)S(1)} %get-tuple-element.40.right_ref), kind=kOutput, calls=%fused_computation | convolution fusion | flops 943194112 | bytes 5636096 | tf_op jit(solution)/shard_map/dot_general | solution.py:29
  150.6 3.9 %all-to-all-done.3.sums_ref = f32[32,1,512]{2,1,0:T(1,128)S(1)} async-done(((f32[32,1,512]{2,1,0:T(1,128)}), f32[32,1,512]{2,1,0:T(1,128)S(1)}, u32[]{:S(2)}, u32[]{:S(2)}) %all-to-all-start.3) | async-done | bytes 65568 | tf_op jit(solution)/shard_map/all_to_all | solution.py:350
  154.5 3.7 %shard_map.62 = (bf16[1024,896]{1,0:T(8,128)(2,1)}, f32[64,896]{1,0:T(8,128)}) custom-call(s32[5]{0:T(128)S(1)} %stack.203.place_ref, bf16[1024,512]{1,0:T(8,128)(2,1)S(1)} %add_convert_fusion.1.left_ref, bf16[512,896]{1,0:T(8,128)(2,1)S(1)} %get-tuple-element.40.right_ref, f32[64,896]{1,0:T(8,128)S(1)} %get-tuple-element.41.own_ref, ...), custom_call_target="tpu_custom_call" | custom-call | flops 939524096 | bytes 4194304 | tf_op jit(solution)/shard_map/pallas_call | solution.py:255
  (58 shorter events, 7.4 us)
Async XLA Ops:
  1.6 11.6 %collective-permute-start.3 = (bf16[64,896]{1,0:T(8,128)(2,1)S(1)}, bf16[64,896]{1,0:T(8,128)(2,1)S(1)}, u32[]{:S(2)}, u32[]{:S(2)}) collective-permute-start(bf16[64,896]{1,0:T(8,128)(2,1)S(1)} %convert_bitcast_fusion.refs_0_), channel_id=1, source_target_pairs={{0,128},{128,0},{1,129},{129,1},{2,130},{130,2},{3,131},{131,3},{4... | collective-permute-start | bytes 344072 | tf_op jit(solution)/shard_map/ppermute | solution.py:277
  9.4 7.2 %collective-permute-start = (bf16[64,896]{1,0:T(8,128)(2,1)S(1)}, bf16[64,896]{1,0:T(8,128)(2,1)S(1)}, u32[]{:S(2)}, u32[]{:S(2)}) collective-permute-start(bf16[64,896]{1,0:T(8,128)(2,1)S(1)} %convert_bitcast_fusion.refs_0_), channel_id=1, source_target_pairs={{0,96},{32,0},{64,32},{96,64},{1,97},{33,1},{65,33},{97,65},{2,98}... | collective-permute-start | bytes 344072 | tf_op jit(solution)/shard_map/ppermute | solution.py:277
  12.1 8.3 %collective-permute-start.1 = (bf16[64,896]{1,0:T(8,128)(2,1)S(1)}, bf16[64,896]{1,0:T(8,128)(2,1)S(1)}, u32[]{:S(2)}, u32[]{:S(2)}) collective-permute-start(bf16[64,896]{1,0:T(8,128)(2,1)S(1)} %convert_bitcast_fusion.refs_0_), channel_id=1, source_target_pairs={{0,64},{32,96},{64,0},{96,32},{1,65},{33,97},{65,1},{97,33},{2,66}... | collective-permute-start | bytes 344072 | tf_op jit(solution)/shard_map/ppermute | solution.py:277
  12.5 9.1 %collective-permute-start.2 = (bf16[64,896]{1,0:T(8,128)(2,1)S(1)}, bf16[64,896]{1,0:T(8,128)(2,1)S(1)}, u32[]{:S(2)}, u32[]{:S(2)}) collective-permute-start(bf16[64,896]{1,0:T(8,128)(2,1)S(1)} %convert_bitcast_fusion.refs_0_), channel_id=1, source_target_pairs={{0,32},{32,64},{64,96},{96,0},{1,33},{33,65},{65,97},{97,1},{2,34}... | collective-permute-start | bytes 344072 | tf_op jit(solution)/shard_map/ppermute | solution.py:277
  13.2 8.4 %collective-permute-start.4 = (bf16[64,896]{1,0:T(8,128)(2,1)S(1)}, bf16[64,896]{1,0:T(8,128)(2,1)S(1)}, u32[]{:S(2)}, u32[]{:S(2)}) collective-permute-start(bf16[64,896]{1,0:T(8,128)(2,1)S(1)} %collective-permute-done.3.refs_4_), channel_id=1, source_target_pairs={{0,96},{32,0},{64,32},{96,64},{1,97},{33,1},{65,33},{97,65},{2,98}... | collective-permute-start | bytes 344072 | tf_op jit(solution)/shard_map/ppermute | solution.py:277
  15.2 6.5 %collective-permute-start.5 = (bf16[64,896]{1,0:T(8,128)(2,1)S(1)}, bf16[64,896]{1,0:T(8,128)(2,1)S(1)}, u32[]{:S(2)}, u32[]{:S(2)}) collective-permute-start(bf16[64,896]{1,0:T(8,128)(2,1)S(1)} %collective-permute-done.3.refs_4_), channel_id=1, source_target_pairs={{0,64},{32,96},{64,0},{96,32},{1,65},{33,97},{65,1},{97,33},{2,66}... | collective-permute-start | bytes 344072 | tf_op jit(solution)/shard_map/ppermute | solution.py:277
  16.6 7.8 %collective-permute-start.6 = (bf16[64,896]{1,0:T(8,128)(2,1)S(1)}, bf16[64,896]{1,0:T(8,128)(2,1)S(1)}, u32[]{:S(2)}, u32[]{:S(2)}) collective-permute-start(bf16[64,896]{1,0:T(8,128)(2,1)S(1)} %collective-permute-done.3.refs_4_), channel_id=1, source_target_pairs={{0,32},{32,64},{64,96},{96,0},{1,33},{33,65},{65,97},{97,1},{2,34}... | collective-permute-start | bytes 344072 | tf_op jit(solution)/shard_map/ppermute | solution.py:277
  20.4 4.6 %copy-start = (bf16[1024,896]{1,0:T(8,128)(2,1)S(1)}, bf16[1024,896]{1,0:T(8,128)(2,1)}, u32[]{:S(2)}) copy-start(bf16[1024,896]{1,0:T(8,128)(2,1)} %add_convert_fusion) | copy-start | bytes 5505028
  25.8 4.2 %collective-permute-start.7 = (bf16[512,512]{1,0:T(8,128)(2,1)S(1)}, bf16[512,512]{1,0:T(8,128)(2,1)S(1)}, u32[]{:S(2)}, u32[]{:S(2)}) collective-permute-start(bf16[512,512]{1,0:T(8,128)(2,1)S(1)} %convolution_convert_fusion.1), channel_id=1, source_target_pairs={{0,1},{1,0},{2,3},{3,2},{4,5},{5,4},{6,7},{7,6},{8,9},{9,8},{10,11... | collective-permute-start | bytes 1572872 | tf_op jit(solution)/shard_map/ppermute | solution.py:277
  30.2 6.3 %collective-permute-start.10 = (bf16[128,512]{1,0:T(8,128)(2,1)S(1)}, bf16[128,512]{1,0:T(8,128)(2,1)S(1)}, u32[]{:S(2)}, u32[]{:S(2)}) collective-permute-start(bf16[128,512]{1,0:T(8,128)(2,1)S(1)} %get-tuple-element.50), channel_id=1, source_target_pairs={{0,8},{8,16},{16,24},{24,0},{1,9},{9,17},{17,25},{25,1},{2,10},{10... | collective-permute-start | bytes 393224 | tf_op jit(solution)/shard_map/ppermute | solution.py:277
  31.5 8.8 %collective-permute-start.9 = (bf16[128,512]{1,0:T(8,128)(2,1)S(1)}, bf16[128,512]{1,0:T(8,128)(2,1)S(1)}, u32[]{:S(2)}, u32[]{:S(2)}) collective-permute-start(bf16[128,512]{1,0:T(8,128)(2,1)S(1)} %get-tuple-element.51), channel_id=1, source_target_pairs={{0,16},{8,24},{16,0},{24,8},{1,17},{9,25},{17,1},{25,9},{2,18},{10... | collective-permute-start | bytes 393224 | tf_op jit(solution)/shard_map/ppermute | solution.py:277
  33.9 6.4 %collective-permute-start.8 = (bf16[128,512]{1,0:T(8,128)(2,1)S(1)}, bf16[128,512]{1,0:T(8,128)(2,1)S(1)}, u32[]{:S(2)}, u32[]{:S(2)}) collective-permute-start(bf16[128,512]{1,0:T(8,128)(2,1)S(1)} %get-tuple-element.49), channel_id=1, source_target_pairs={{0,24},{8,0},{16,8},{24,16},{1,25},{9,1},{17,9},{25,17},{2,26},{10... | collective-permute-start | bytes 393224 | tf_op jit(solution)/shard_map/ppermute | solution.py:277
  40.4 4.8 %collective-permute-start.13 = (bf16[32,512]{1,0:T(8,128)(2,1)S(1)}, bf16[32,512]{1,0:T(8,128)(2,1)S(1)}, u32[]{:S(2)}, u32[]{:S(2)}) collective-permute-start(bf16[32,512]{1,0:T(8,128)(2,1)S(1)} %get-tuple-element.53), channel_id=1, source_target_pairs={{0,2},{2,4},{4,6},{6,0},{1,3},{3,5},{5,7},{7,1},{8,10},{10,12},{12... | collective-permute-start | bytes 98312 | tf_op jit(solution)/shard_map/ppermute | solution.py:277
  41.3 4.0 %collective-permute-start.12 = (bf16[32,512]{1,0:T(8,128)(2,1)S(1)}, bf16[32,512]{1,0:T(8,128)(2,1)S(1)}, u32[]{:S(2)}, u32[]{:S(2)}) collective-permute-start(bf16[32,512]{1,0:T(8,128)(2,1)S(1)} %get-tuple-element.54), channel_id=1, source_target_pairs={{0,4},{2,6},{4,0},{6,2},{1,5},{3,7},{5,1},{7,3},{8,12},{10,14},{12... | collective-permute-start | bytes 98312 | tf_op jit(solution)/shard_map/ppermute | solution.py:277
  42.6 3.3 %collective-permute-start.11 = (bf16[32,512]{1,0:T(8,128)(2,1)S(1)}, bf16[32,512]{1,0:T(8,128)(2,1)S(1)}, u32[]{:S(2)}, u32[]{:S(2)}) collective-permute-start(bf16[32,512]{1,0:T(8,128)(2,1)S(1)} %get-tuple-element.52), channel_id=1, source_target_pairs={{0,6},{2,0},{4,2},{6,4},{1,7},{3,1},{5,3},{7,5},{8,14},{10,8},{12,... | collective-permute-start | bytes 98312 | tf_op jit(solution)/shard_map/ppermute | solution.py:277
  67.6 3.9 %collective-permute-start.14 = (bf16[512,512]{1,0:T(8,128)(2,1)S(1)}, bf16[512,512]{1,0:T(8,128)(2,1)S(1)}, u32[]{:S(2)}, u32[]{:S(2)}) collective-permute-start(bf16[512,512]{1,0:T(8,128)(2,1)S(1)} %bitcast.68), channel_id=1, source_target_pairs={{0,1},{1,0},{2,3},{3,2},{4,5},{5,4},{6,7},{7,6},{8,9},{9,8},{10,11... | collective-permute-start | bytes 1572872 | tf_op jit(solution)/shard_map/ppermute | solution.py:277
  72.9 15.7 %all-to-all-start.1 = ((f32[8,40,128]{2,1,0:T(8,128)}), f32[8,40,128]{2,1,0:T(8,128)S(1)}, u32[]{:S(2)}, u32[]{:S(2)}) async-start(f32[8,40,128]{2,1,0:T(8,128)} %broadcast_in_dim.7), calls=%async_computation.1 | async-start | bytes 327680 | tf_op jit(solution)/shard_map/all_to_all | solution.py:272
  82.5 10.0 %collective-permute-start.15 = (bf16[128,896]{1,0:T(8,128)(2,1)S(1)}, bf16[128,896]{1,0:T(8,128)(2,1)S(1)}, u32[]{:S(2)}, u32[]{:S(2)}) collective-permute-start(bf16[128,896]{1,0:T(8,128)(2,1)S(1)} %get-tuple-element.47), channel_id=1, source_target_pairs={{0,96},{32,0},{64,32},{96,64},{1,97},{33,1},{65,33},{97,65},{2,98}... | collective-permute-start | bytes 688136 | tf_op jit(solution)/shard_map/ppermute | solution.py:277
  85.3 8.3 %collective-permute-start.16 = (bf16[128,896]{1,0:T(8,128)(2,1)S(1)}, bf16[128,896]{1,0:T(8,128)(2,1)S(1)}, u32[]{:S(2)}, u32[]{:S(2)}) collective-permute-start(bf16[128,896]{1,0:T(8,128)(2,1)S(1)} %get-tuple-element.46), channel_id=1, source_target_pairs={{0,64},{32,96},{64,0},{96,32},{1,65},{33,97},{65,1},{97,33},{2,66}... | collective-permute-start | bytes 688136 | tf_op jit(solution)/shard_map/ppermute | solution.py:277
  85.8 13.8 %collective-permute-start.17 = (bf16[128,896]{1,0:T(8,128)(2,1)S(1)}, bf16[128,896]{1,0:T(8,128)(2,1)S(1)}, u32[]{:S(2)}, u32[]{:S(2)}) collective-permute-start(bf16[128,896]{1,0:T(8,128)(2,1)S(1)} %get-tuple-element.45), channel_id=1, source_target_pairs={{0,32},{32,64},{64,96},{96,0},{1,33},{33,65},{65,97},{97,1},{2,34}... | collective-permute-start | bytes 688136 | tf_op jit(solution)/shard_map/ppermute | solution.py:277
  89.2 10.5 %all-to-all-start.2 = ((f32[4,40,128]{2,1,0:T(8,128)}), f32[4,40,128]{2,1,0:T(8,128)S(1)}, u32[]{:S(2)}, u32[]{:S(2)}) async-start(f32[4,40,128]{2,1,0:T(8,128)} %broadcast_in_dim.8), calls=%async_computation.2 | async-start | bytes 163840 | tf_op jit(solution)/shard_map/all_to_all | solution.py:272
  99.8 13.3 %collective-permute-start.18 = (bf16[128,896]{1,0:T(8,128)(2,1)S(1)}, bf16[128,896]{1,0:T(8,128)(2,1)S(1)}, u32[]{:S(2)}, u32[]{:S(2)}) collective-permute-start(bf16[128,896]{1,0:T(8,128)(2,1)S(1)} %add_convert_fusion.4), channel_id=1, source_target_pairs={{0,128},{128,0},{1,129},{129,1},{2,130},{130,2},{3,131},{131,3},{4... | collective-permute-start | bytes 688136 | tf_op jit(solution)/shard_map/ppermute | solution.py:277
  104.5 3.6 %collective-permute-start.19 = (f32[160,128]{1,0:T(8,128)S(1)}, f32[160,128]{1,0:T(8,128)S(1)}, u32[]{:S(2)}, u32[]{:S(2)}) collective-permute-start(f32[160,128]{1,0:T(8,128)S(1)} %bitcast.70), channel_id=1, source_target_pairs={{0,24},{8,0},{16,8},{24,16},{1,25},{9,1},{17,9},{25,17},{2,26},{10... | collective-permute-start | bytes 245768 | tf_op jit(solution)/shard_map/ppermute | solution.py:277
  105.1 5.1 %collective-permute-start.20 = (f32[160,128]{1,0:T(8,128)S(1)}, f32[160,128]{1,0:T(8,128)S(1)}, u32[]{:S(2)}, u32[]{:S(2)}) collective-permute-start(f32[160,128]{1,0:T(8,128)S(1)} %bitcast.71), channel_id=1, source_target_pairs={{0,16},{8,24},{16,0},{24,8},{1,17},{9,25},{17,1},{25,9},{2,18},{10... | collective-permute-start | bytes 245768 | tf_op jit(solution)/shard_map/ppermute | solution.py:277
  105.4 6.0 %collective-permute-start.21 = (f32[160,128]{1,0:T(8,128)S(1)}, f32[160,128]{1,0:T(8,128)S(1)}, u32[]{:S(2)}, u32[]{:S(2)}) collective-permute-start(f32[160,128]{1,0:T(8,128)S(1)} %bitcast.72), channel_id=1, source_target_pairs={{0,8},{8,16},{16,24},{24,0},{1,9},{9,17},{17,25},{25,1},{2,10},{10... | collective-permute-start | bytes 245768 | tf_op jit(solution)/shard_map/ppermute | solution.py:277
  113.2 5.0 %collective-permute-start.22 = (f32[640,128]{1,0:T(8,128)S(1)}, f32[640,128]{1,0:T(8,128)S(1)}, u32[]{:S(2)}, u32[]{:S(2)}) collective-permute-start(f32[640,128]{1,0:T(8,128)S(1)} %constant_dynamic-update-slice_fusion.own_ref), channel_id=1, source_target_pairs={{0,1},{1,0},{2,3},{3,2},{4,5},{5,4},{6,7},{7,6},{8,9},{9,8},{10,11... | collective-permute-start | bytes 983048 | tf_op jit(solution)/shard_map/ppermute | solution.py:277
  118.2 21.3 %collective-permute-start.23 = (bf16[128,896]{1,0:T(8,128)(2,1)S(1)}, bf16[128,896]{1,0:T(8,128)(2,1)S(1)}, u32[]{:S(2)}, u32[]{:S(2)}) collective-permute-start(bf16[128,896]{1,0:T(8,128)(2,1)S(1)} %add_convert_fusion.3.refs_0_), channel_id=1, source_target_pairs={{0,96},{32,0},{64,32},{96,64},{1,97},{33,1},{65,33},{97,65},{2,98}... | collective-permute-start | bytes 688136 | tf_op jit(solution)/shard_map/ppermute | solution.py:277
  118.2 21.3 %collective-permute-start.24 = (bf16[128,896]{1,0:T(8,128)(2,1)S(1)}, bf16[128,896]{1,0:T(8,128)(2,1)S(1)}, u32[]{:S(2)}, u32[]{:S(2)}) collective-permute-start(bf16[128,896]{1,0:T(8,128)(2,1)S(1)} %add_convert_fusion.3.refs_0_), channel_id=1, source_target_pairs={{0,64},{32,96},{64,0},{96,32},{1,65},{33,97},{65,1},{97,33},{2,66}... | collective-permute-start | bytes 688136 | tf_op jit(solution)/shard_map/ppermute | solution.py:277
  118.2 21.3 %collective-permute-start.25 = (bf16[128,896]{1,0:T(8,128)(2,1)S(1)}, bf16[128,896]{1,0:T(8,128)(2,1)S(1)}, u32[]{:S(2)}, u32[]{:S(2)}) collective-permute-start(bf16[128,896]{1,0:T(8,128)(2,1)S(1)} %add_convert_fusion.3.refs_0_), channel_id=1, source_target_pairs={{0,32},{32,64},{64,96},{96,0},{1,33},{33,65},{65,97},{97,1},{2,34}... | collective-permute-start | bytes 688136 | tf_op jit(solution)/shard_map/ppermute | solution.py:277
  142.1 12.3 %all-to-all-start.3 = ((f32[32,1,512]{2,1,0:T(1,128)}), f32[32,1,512]{2,1,0:T(1,128)S(1)}, u32[]{:S(2)}, u32[]{:S(2)}) async-start(f32[32,1,512]{2,1,0:T(1,128)} %get-tuple-element.42), calls=%async_computation.3 | async-start | bytes 131072 | tf_op jit(solution)/shard_map/all_to_all | solution.py:350

commit v2 on v1

--- a/solution.py
+++ b/solution.py
@@ -196,22 +196,25 @@
 
 
 def right_kernel(place_ref, high_ref, low_ref, *refs):
-    pieces, (right_ref, own_ref, sums_ref, raw, whole) = refs[:4], refs[4:]
+    pieces, (right_ref, own_ref, sums_ref, raw) = refs[:4], refs[4:]
     quarter = R // 4
     for n in range(4):
         into = pl.multiple_of(place_ref[n] * quarter, quarter)
         raw[pl.ds(into, quarter), :] = pieces[n][...]
-    for lo in range(0, R, BLOCK):
-        band = slice(lo, lo + BLOCK)
-        right = product(high_ref[band, :], raw[...], 1, 0) + product(low_ref[band, :], raw[...], 1, 0)
-        whole[band, :] = right
-        right_ref[band, :] = right.astype(bf16)
+    rows = own_ref.shape[0]
+    mine = pl.ds(pl.multiple_of(place_ref[4] * rows, rows), rows)
+    both = jnp.concatenate([high_ref[...], low_ref[...], high_ref[mine, :], low_ref[mine, :]])
+    folded = []
+    for lo in range(0, raw.shape[1], 2 * BLOCK):
+        band = slice(lo, min(lo + 2 * BLOCK, raw.shape[1]))
+        parts = product(both, raw[:, band], 1, 0)
+        right = parts[:R, :] + parts[R : 2 * R, :]
+        right_ref[:, band] = right.astype(bf16)
+        own_ref[:, band] = parts[2 * R : 2 * R + rows, :] + parts[2 * R + rows :, :]
         square = right * right
-        folded = added([square[:, at : at + BLOCK] for at in range(0, right.shape[1], BLOCK)])
-        row = jnp.sum(folded.T, axis=0, keepdims=True)
-        sums_ref[:, :, band] = jnp.broadcast_to(row[None], (2 * FAR, 1, BLOCK))
-    rows = own_ref.shape[0]
-    own_ref[...] = whole[pl.ds(pl.multiple_of(place_ref[4] * rows, rows), rows), :]
+        folded += [square[:, at : at + BLOCK] for at in range(0, right.shape[1], BLOCK)]
+    row = jnp.sum(added(folded).T, axis=0, keepdims=True)
+    sums_ref[...] = jnp.broadcast_to(row[None], sums_ref.shape)
 
 
 def right_side(place, high, low, pieces, rows):
@@ -225,32 +228,33 @@
             jax.ShapeDtypeStruct((rows, width), f32),
             jax.ShapeDtypeStruct((2 * FAR, 1, R), f32),
         ],
-        [((R, width), bf16), ((R, width), f32)],
+        [((R, width), bf16)],
         4 * R * R * width,
     )
 
 
-def update_kernel(place_ref, left_ref, right_ref, own_ref, sums_ref, update_ref, factor_ref, inverse, column):
+def update_kernel(place_ref, left_ref, right_ref, own_ref, sums_ref, update_ref, factor_ref, inverse):
     step = pl.program_id(0)
 
     @pl.when(step == 0)
     def _():
-        inverse[...] = lax.rsqrt(jnp.sum(sums_ref[...], axis=0) + epsilon)
-        column[...] = jnp.broadcast_to(inverse[...], (BLOCK, R)).T
+        norms = lax.rsqrt(jnp.sum(sums_ref[...], axis=0) + epsilon)
+        inverse[...] = norms * math.sqrt(D * FF / R)
         rows = own_ref.shape[0]
-        scale = column[pl.ds(pl.multiple_of(place_ref[4] * rows, rows), rows), :]
-        for at in range(0, own_ref.shape[1], BLOCK):
-            factor_ref[:, at : at + BLOCK] = own_ref[:, at : at + BLOCK] * scale
+        lane = lax.broadcasted_iota(jnp.int32, (rows, R), 1)
+        row = lax.broadcasted_iota(jnp.int32, (rows, R), 0) + place_ref[4] * rows
+        scale = jnp.sum(jnp.where(lane == row, norms, 0.0), axis=1, keepdims=True)
+        factor_ref[...] = own_ref[...] * scale
 
     band = update_ref.shape[0]
     left = left_ref[pl.ds(pl.multiple_of(step * band, band), band), :]
     scaled = (left.astype(f32) * inverse[...]).astype(bf16)
-    update_ref[...] = (product(scaled, right_ref[...], 1, 0) * math.sqrt(D * FF / R)).astype(bf16)
+    update_ref[...] = product(scaled, right_ref[...], 1, 0).astype(bf16)
 
 
 def update_side(place, left, right, own, sums):
     height, width = left.shape[0], right.shape[1]
-    steps = 4
+    steps = 2
     whole = pl.BlockSpec(memory_space=pltpu.VMEM)
     return pl.pallas_call(
         update_kernel,
@@ -261,7 +265,7 @@
             pl.BlockSpec((height // steps, width), lambda i: (i, 0)),
             pl.BlockSpec(own.shape, lambda i: (0, 0)),
         ],
-        scratch_shapes=[pltpu.VMEM((1, R), f32), pltpu.VMEM((R, BLOCK), f32)],
+        scratch_shapes=[pltpu.VMEM((1, R), f32)],
         compiler_params=pltpu.CompilerParams(vmem_limit_bytes=12 << 20),
         cost_estimate=pl.CostEstimate(flops=2 * R * height * width, bytes_accessed=4 << 20, transcendentals=0),
     )(place, left, right, own, sums)
@@ -298,7 +302,7 @@
     gram_place = jnp.stack(
         [(core + c) % 2 * FAR + (x + j) % 4 * 4 + i for c in range(2) for j in range(4) for i in range(4)]
     ).astype(jnp.int32)
-    core_place = jnp.stack([core, 1 - core]).astype(jnp.int32)
+    left_place = jnp.stack([(core + c) % 2 * 4 + (x + j) % 4 for c in range(2) for j in range(4)]).astype(jnp.int32)
     fsdp_place = jnp.stack([(z_hi + h) % 2 * 4 + (y + k) % 4 for h in range(2) for k in range(4)]).astype(jnp.int32)
     row_group = z_hi * 4 + y
     right_place = jnp.stack([(y + k) % 4 for k in range(4)] + [row_group]).astype(jnp.int32)
@@ -318,7 +322,8 @@
     partial_left = (kept + arrived.astype(f32)).astype(bf16)
     left_line = total(exchanged(partial_left, "x", x)).astype(bf16)
     left_rows = total(exchanged(left_line, "z_lo", z_lo)).astype(bf16)
-    own_left = from_everyone(left_rows, ("x", "z_lo")).reshape(half, R)
+    left_line = from_everyone(left_rows, "z_lo").reshape(half // 4, R)
+    own_left = jnp.concatenate(ahead(left_line, "x"))
     other_left = from_ahead(own_left, "core", 1)
 
     local_gram = product(own_left, own_left, 0, 0) + product(other_left, other_left, 0, 0)
@@ -328,7 +333,7 @@
     piece = lax.dynamic_slice_in_dim(packed, (core * FAR + x * 4 + z_lo) * SHARE, SHARE, 0)
     summed = jnp.sum(from_everyone(piece, ("z_hi", "y")), axis=0)
 
-    left_factor = arrange(core_place, (own_left, other_left), half)
+    left_factor = arrange(left_place, (own_left, other_left), half // 4)
     partial_right = product(left_factor, blended, 0, 0).astype(bf16)
     received = exchanged(partial_right, "y", y)
 

time: 159 us -> 158 us (level)
  blocking collectives: 21.7 us -> 9.39 us
  starting transfers between devices: 58.1 us -> 70.2 us
    all_to_all x1, blocking collectives: 21.7 us -> 9.39 us  [from_everyone(): lax.all_to_all(jnp.broadcast_to(value[None], (length, *value.shape)), axi...]
    ppermute x26 -> x29, starting transfers between devices: 44.2 us -> 52 us  [from_ahead(): lax.ppermute(value, axis, [(i, (i - steps) % length) for i in range(lengt...]
    all_to_all x1, starting transfers between devices: 4.44 us -> 7.6 us  [on_device(): sums = lax.all_to_all(own_sums, TENSOR, 0, 0, tiled=True)]
    ppermute x26 -> x29, waiting for transfers between devices: 26.5 us -> 26.8 us  [from_ahead(): lax.ppermute(value, axis, [(i, (i - steps) % length) for i in range(lengt...]
  transfers between devices with their start and end apart: 29 -> 32, of which waited for: 18 -> 19; matrix products, arithmetic and copies ran while one was open for 10% -> 10% of each run, Pallas kernels for 12% -> 12%
where the time goes in v2:
time: 158 us
  starting transfers between devices  70.2 us (44%)
  waiting for transfers between devices  32.8 us (21%)
  Pallas kernels  25.3 us (16%)
  matrix products  11.9 us (8%)
  blocking collectives  9.39 us (6%)
  other arithmetic  5.17 us (3%)
  local copies, waits for them, and re-layouts  1.99 us (1%)
    ppermute x29, starting transfers between devices, from_ahead(): lax.ppermute(value, axis, [(i, (i - steps) % length) for i in range(lengt...  52 us
    ppermute x29, waiting for transfers between devices, from_ahead(): lax.ppermute(value, axis, [(i, (i - steps) % length) for i in range(lengt...  26.8 us
    pallas_call x4, Pallas kernels, kernel_call(): pl.pallas_call(kernel, out_shape=outputs, in_specs=[pl.BlockSpec(memory_s...  22.2 us
    dot_general x8, matrix products, product(): lax.dot_general(left, right, (((left_dim,), (right_dim,)), ((), ())), pre...  11.9 us
    all_to_all x2, starting transfers between devices, from_everyone(): lax.all_to_all(jnp.broadcast_to(value[None], (length, *value.shape)), axi...  10.6 us
    all_to_all x1, blocking collectives, from_everyone(): lax.all_to_all(jnp.broadcast_to(value[None], (length, *value.shape)), axi...  9.39 us
    all_to_all x1, starting transfers between devices, on_device(): sums = lax.all_to_all(own_sums, TENSOR, 0, 0, tiled=True)  7.6 us
    all_to_all x1, waiting for transfers between devices, on_device(): sums = lax.all_to_all(own_sums, TENSOR, 0, 0, tiled=True)  3.77 us
  transfers between devices with their start and end apart: 32, of which 19 were waited for; matrix products, arithmetic and copies ran while one was open for 10% of the time, Pallas kernels for 12%

profile of v2, /device:TPU:1, one launch (start us, length us, event | category | flops | bytes accessed | tf_op | source)
XLA Modules:
  0.0 157.6 jit_solution(6971092265842022957)
XLA Ops:
  0.6 1.0 convert_bitcast_fusion.refs_0_
  1.6 7.8 %collective-permute-start.3 = (bf16[64,896]{1,0:T(8,128)(2,1)S(1)}, bf16[64,896]{1,0:T(8,128)(2,1)S(1)}, u32[]{:S(2)}, u32[]{:S(2)}) collective-permute-start(bf16[64,896]{1,0:T(8,128)(2,1)S(1)} %convert_bitcast_fusion.refs_0_), channel_id=1, source_target_pairs={{0,128},{128,0},{1,129},{129,1},{2,130},{130,2},{3,131},{131,3},{4... | collective-permute-start | bytes 344072 | tf_op jit(solution)/shard_map/ppermute | solution.py:281
  9.4 2.7 %collective-permute-start = (bf16[64,896]{1,0:T(8,128)(2,1)S(1)}, bf16[64,896]{1,0:T(8,128)(2,1)S(1)}, u32[]{:S(2)}, u32[]{:S(2)}) collective-permute-start(bf16[64,896]{1,0:T(8,128)(2,1)S(1)} %convert_bitcast_fusion.refs_0_), channel_id=1, source_target_pairs={{0,96},{32,0},{64,32},{96,64},{1,97},{33,1},{65,33},{97,65},{2,98}... | collective-permute-start | bytes 344072 | tf_op jit(solution)/shard_map/ppermute | solution.py:281
  13.2 2.0 %collective-permute-start.4 = (bf16[64,896]{1,0:T(8,128)(2,1)S(1)}, bf16[64,896]{1,0:T(8,128)(2,1)S(1)}, u32[]{:S(2)}, u32[]{:S(2)}) collective-permute-start(bf16[64,896]{1,0:T(8,128)(2,1)S(1)} %collective-permute-done.3.refs_4_), channel_id=1, source_target_pairs={{0,96},{32,0},{64,32},{96,64},{1,97},{33,1},{65,33},{97,65},{2,98}... | collective-permute-start | bytes 344072 | tf_op jit(solution)/shard_map/ppermute | solution.py:281
  15.2 1.4 collective-permute-start.5
  16.6 3.7 %add_convert_fusion = bf16[1024,896]{1,0:T(8,128)(2,1)} fusion(bf16[1024,896]{1,0:T(8,128)(2,1)} %param.4, bf16[1024,896]{1,0:T(8,128)(2,1)} %param.3), kind=kLoop, calls=%fused_computation.1 | loop fusion | flops 3670016 | bytes 5505024 | tf_op jit(solution)/shard_map/convert_element_type | solution.py:314
  20.4 1.1 collective-permute-done.2.refs_3_
  21.7 2.8 %collective-permute-done.6.refs_7_ = bf16[64,896]{1,0:T(8,128)(2,1)S(1)} collective-permute-done((bf16[64,896]{1,0:T(8,128)(2,1)S(1)}, bf16[64,896]{1,0:T(8,128)(2,1)S(1)}, u32[]{:S(2)}, u32[]{:S(2)}) %collective-permute-start.6) | collective-permute-done | bytes 114720 | tf_op jit(solution)/shard_map/ppermute | solution.py:281
  25.1 0.7 convolution_convert_fusion.1
  25.8 2.2 %collective-permute-start.7 = (bf16[512,512]{1,0:T(8,128)(2,1)S(1)}, bf16[512,512]{1,0:T(8,128)(2,1)S(1)}, u32[]{:S(2)}, u32[]{:S(2)}) collective-permute-start(bf16[512,512]{1,0:T(8,128)(2,1)S(1)} %convolution_convert_fusion.1), channel_id=1, source_target_pairs={{0,1},{1,0},{2,3},{3,2},{4,5},{5,4},{6,7},{7,6},{8,9},{9,8},{10,11... | collective-permute-start | bytes 1572872 | tf_op jit(solution)/shard_map/ppermute | solution.py:281
  28.1 1.9 %fusion.1 = f32[512,512]{1,0:T(8,128)S(1)} fusion(bf16[512,896]{1,0:T(8,128)(2,1)S(1)} %shard_map.58, bf16[1024,896]{1,0:T(8,128)(2,1)} %add_convert_fusion, s32[]{:T(128)S(6)} %select_n.310), kind=kOutput, calls=%fused_computation.8 | convolution fusion | flops 469762048 | bytes 2883588 | tf_op jit(solution)/shard_map/dot_general | solution.py:29
  30.2 1.3 collective-permute-start.10
  31.5 2.5 %collective-permute-start.9 = (bf16[128,512]{1,0:T(8,128)(2,1)S(1)}, bf16[128,512]{1,0:T(8,128)(2,1)S(1)}, u32[]{:S(2)}, u32[]{:S(2)}) collective-permute-start(bf16[128,512]{1,0:T(8,128)(2,1)S(1)} %get-tuple-element.51), channel_id=1, source_target_pairs={{0,16},{8,24},{16,0},{24,8},{1,17},{9,25},{17,1},{25,9},{2,18},{10... | collective-permute-start | bytes 393224 | tf_op jit(solution)/shard_map/ppermute | solution.py:281
  33.9 1.2 collective-permute-start.8
  35.1 1.4 collective-permute-done.10
  36.5 3.8 %collective-permute-done.9 = bf16[128,512]{1,0:T(8,128)(2,1)S(1)} collective-permute-done((bf16[128,512]{1,0:T(8,128)(2,1)S(1)}, bf16[128,512]{1,0:T(8,128)(2,1)S(1)}, u32[]{:S(2)}, u32[]{:S(2)}) %collective-permute-start.9) | collective-permute-done | bytes 131104 | tf_op jit(solution)/shard_map/ppermute | solution.py:281
  40.4 0.8 collective-permute-start.13
  41.3 1.3 collective-permute-start.12
  42.6 2.3 %collective-permute-start.11 = (bf16[32,512]{1,0:T(8,128)(2,1)S(1)}, bf16[32,512]{1,0:T(8,128)(2,1)S(1)}, u32[]{:S(2)}, u32[]{:S(2)}) collective-permute-start(bf16[32,512]{1,0:T(8,128)(2,1)S(1)} %get-tuple-element.52), channel_id=1, source_target_pairs={{0,6},{2,0},{4,2},{6,4},{1,7},{3,1},{5,3},{7,5},{8,14},{10,8},{12,... | collective-permute-start | bytes 98312 | tf_op jit(solution)/shard_map/ppermute | solution.py:281
  45.9 9.4 %all_to_all.20 = bf16[4,32,512]{2,1,0:T(8,128)(2,1)S(1)} all-to-all(bf16[4,32,512]{2,1,0:T(8,128)(2,1)S(1)} %broadcast_in_dim.6), channel_id=1, replica_groups=mesh['z_hi'=2,'y'=4,'x'=4,'z_lo'=4,'core'=2] {'z_lo'}, dimensions={0} | all-to-all | bytes 262144 | tf_op jit(solution)/shard_map/all_to_all | solution.py:276
  55.3 0.8 collective-permute-start.16
  56.1 2.3 %collective-permute-start.15 = (bf16[128,512]{1,0:T(8,128)(2,1)S(1)}, bf16[128,512]{1,0:T(8,128)(2,1)S(1)}, u32[]{:S(2)}, u32[]{:S(2)}) collective-permute-start(bf16[128,512]{1,0:T(8,128)(2,1)S(1)} %bitcast.71), channel_id=1, source_target_pairs={{0,16},{8,24},{16,0},{24,8},{1,17},{9,25},{17,1},{25,9},{2,18},{10... | collective-permute-start | bytes 393224 | tf_op jit(solution)/shard_map/ppermute | solution.py:281
  58.5 1.1 collective-permute-start.14
  59.5 0.8 collective-permute-done.16
  60.3 1.9 %collective-permute-done.15 = bf16[128,512]{1,0:T(8,128)(2,1)S(1)} collective-permute-done((bf16[128,512]{1,0:T(8,128)(2,1)S(1)}, bf16[128,512]{1,0:T(8,128)(2,1)S(1)}, u32[]{:S(2)}, u32[]{:S(2)}) %collective-permute-start.15) | collective-permute-done | bytes 131104 | tf_op jit(solution)/shard_map/ppermute | solution.py:281
  62.3 5.8 %collective-permute-start.17 = (bf16[512,512]{1,0:T(8,128)(2,1)S(1)}, bf16[512,512]{1,0:T(8,128)(2,1)S(1)}, u32[]{:S(2)}, u32[]{:S(2)}) collective-permute-start(bf16[512,512]{1,0:T(8,128)(2,1)S(1)} %pad_maximum_fusion.refs_0_), channel_id=1, source_target_pairs={{0,1},{1,0},{2,3},{3,2},{4,5},{5,4},{6,7},{7,6},{8,9},{9,8},{10,11... | collective-permute-start | bytes 1572872 | tf_op jit(solution)/shard_map/ppermute | solution.py:281
  68.2 1.5 collective-permute-done.17.refs_1_
  71.5 6.2 %all-to-all-start.1 = ((f32[8,40,128]{2,1,0:T(8,128)}), f32[8,40,128]{2,1,0:T(8,128)S(1)}, u32[]{:S(2)}, u32[]{:S(2)}) async-start(f32[8,40,128]{2,1,0:T(8,128)} %broadcast_in_dim.7), calls=%async_computation.1 | async-start | bytes 327680 | tf_op jit(solution)/shard_map/all_to_all | solution.py:276
  78.3 2.8 %convolution_convert_fusion = bf16[512,896]{1,0:T(8,128)(2,1)S(1)} fusion(bf16[1024,512]{1,0:T(8,128)(2,1)S(1)} %shard_map.59, bf16[1024,896]{1,0:T(8,128)(2,1)} %add_convert_fusion), kind=kOutput, calls=%fused_computation.3 | convolution fusion | flops 939982848 | bytes 3801088 | tf_op jit(solution)/shard_map/dot_general | solution.py:29
  81.2 2.7 %collective-permute-start.18 = (bf16[128,896]{1,0:T(8,128)(2,1)S(1)}, bf16[128,896]{1,0:T(8,128)(2,1)S(1)}, u32[]{:S(2)}, u32[]{:S(2)}) collective-permute-start(bf16[128,896]{1,0:T(8,128)(2,1)S(1)} %get-tuple-element.47), channel_id=1, source_target_pairs={{0,96},{32,0},{64,32},{96,64},{1,97},{33,1},{65,33},{97,65},{2,98}... | collective-permute-start | bytes 688136 | tf_op jit(solution)/shard_map/ppermute | solution.py:281
  85.1 2.2 %all-to-all-done.1 = f32[8,40,128]{2,1,0:T(8,128)S(1)} async-done(((f32[8,40,128]{2,1,0:T(8,128)}), f32[8,40,128]{2,1,0:T(8,128)S(1)}, u32[]{:S(2)}, u32[]{:S(2)}) %all-to-all-start.1) | async-done | bytes 163872 | tf_op jit(solution)/shard_map/all_to_all | solution.py:276
  87.9 4.4 %all-to-all-start.2 = ((f32[4,40,128]{2,1,0:T(8,128)}), f32[4,40,128]{2,1,0:T(8,128)S(1)}, u32[]{:S(2)}, u32[]{:S(2)}) async-start(f32[4,40,128]{2,1,0:T(8,128)} %broadcast_in_dim.8), calls=%async_computation.2 | async-start | bytes 163840 | tf_op jit(solution)/shard_map/all_to_all | solution.py:276
  92.3 5.9 %collective-permute-done.20 = bf16[128,896]{1,0:T(8,128)(2,1)S(1)} collective-permute-done((bf16[128,896]{1,0:T(8,128)(2,1)S(1)}, bf16[128,896]{1,0:T(8,128)(2,1)S(1)}, u32[]{:S(2)}, u32[]{:S(2)}) %collective-permute-start.20) | collective-permute-done | bytes 229408 | tf_op jit(solution)/shard_map/ppermute | solution.py:281
  98.4 4.7 %collective-permute-start.21 = (bf16[128,896]{1,0:T(8,128)(2,1)S(1)}, bf16[128,896]{1,0:T(8,128)(2,1)S(1)}, u32[]{:S(2)}, u32[]{:S(2)}) collective-permute-start(bf16[128,896]{1,0:T(8,128)(2,1)S(1)} %add_convert_fusion.4), channel_id=1, source_target_pairs={{0,128},{128,0},{1,129},{129,1},{2,130},{130,2},{3,131},{131,3},{4... | collective-permute-start | bytes 688136 | tf_op jit(solution)/shard_map/ppermute | solution.py:281
  103.2 2.5 %collective-permute-start.22 = (f32[160,128]{1,0:T(8,128)S(1)}, f32[160,128]{1,0:T(8,128)S(1)}, u32[]{:S(2)}, u32[]{:S(2)}) collective-permute-start(f32[160,128]{1,0:T(8,128)S(1)} %bitcast.75), channel_id=1, source_target_pairs={{0,24},{8,0},{16,8},{24,16},{1,25},{9,1},{17,9},{25,17},{2,26},{10... | collective-permute-start | bytes 245768 | tf_op jit(solution)/shard_map/ppermute | solution.py:281
  105.7 0.8 collective-permute-start.23
  106.4 1.1 collective-permute-done.22
  107.6 3.2 %collective-permute-done.23 = f32[160,128]{1,0:T(8,128)S(1)} collective-permute-done((f32[160,128]{1,0:T(8,128)S(1)}, f32[160,128]{1,0:T(8,128)S(1)}, u32[]{:S(2)}, u32[]{:S(2)}) %collective-permute-start.23) | collective-permute-done | bytes 81952 | tf_op jit(solution)/shard_map/ppermute | solution.py:281
  110.7 1.1 collective-permute-done.24
  111.9 2.1 %collective-permute-start.25 = (f32[640,128]{1,0:T(8,128)S(1)}, f32[640,128]{1,0:T(8,128)S(1)}, u32[]{:S(2)}, u32[]{:S(2)}) collective-permute-start(f32[640,128]{1,0:T(8,128)S(1)} %constant_dynamic-update-slice_fusion.own_ref), channel_id=1, source_target_pairs={{0,1},{1,0},{2,3},{3,2},{4,5},{5,4},{6,7},{7,6},{8,9},{9,8},{10,11... | collective-permute-start | bytes 983048 | tf_op jit(solution)/shard_map/ppermute | solution.py:281
  114.2 1.0 collective-permute-done.25.other_ref
  115.3 1.2 collective-permute-start.27
  116.6 18.3 %shard_map.60 = (bf16[512,512]{1,0:T(8,128)(2,1)S(1)}, bf16[512,512]{1,0:T(8,128)(2,1)S(1)}) custom-call(s32[32]{0:T(128)S(1)} %stack.221.place_ref, f32[640,128]{1,0:T(8,128)S(1)} %constant_dynamic-update-slice_fusion.own_ref, f32[640,128]{1,0:T(8,128)S(1)} %collective-permute-done.25.other_ref), custom_call_target="tpu_custom_call" | custom-call | flops 2684354560 | bytes 2097152 | tf_op jit(solution)/shard_map/pallas_call | solution.py:162
  136.5 2.7 %shard_map.61 = (bf16[512,896]{1,0:T(8,128)(2,1)S(1)}, f32[64,896]{1,0:T(8,128)S(1)}, f32[32,1,512]{2,1,0:T(1,128)}) custom-call(s32[5]{0:T(128)S(1)} %stack.227.place_ref, bf16[512,512]{1,0:T(8,128)(2,1)S(1)} %get-tuple-element.37.high_ref, bf16[512,512]{1,0:T(8,128)(2,1)S(1)} %get-tuple-element.38.low_ref, bf16[128,896]{1,0:T(8,128)(2,1)S(1)} %add_convert_fusion.3.refs_0_, ...), custom_call_target="tpu_custom_call" | custom-call | flops 939524096 | bytes 2097152 | tf_op jit(solution)/shard_map/pallas_call | solution.py:162
  139.2 7.6 %all-to-all-start.3 = ((f32[32,1,512]{2,1,0:T(1,128)}), f32[32,1,512]{2,1,0:T(1,128)S(1)}, u32[]{:S(2)}, u32[]{:S(2)}) async-start(f32[32,1,512]{2,1,0:T(1,128)} %get-tuple-element.42), calls=%async_computation.3 | async-start | bytes 131072 | tf_op jit(solution)/shard_map/all_to_all | solution.py:355
  146.8 4.0 %subtract_convert_fusion = bf16[1024,896]{1,0:T(8,128)(2,1)} fusion(bf16[1024,896]{1,0:T(8,128)(2,1)} %add_convert_fusion, bf16[1024,512]{1,0:T(8,128)(2,1)S(1)} %add_convert_fusion.1.left_ref, bf16[512,896]{1,0:T(8,128)(2,1)S(1)} %get-tuple-element.40.right_ref), kind=kOutput, calls=%fused_computation | convolution fusion | flops 943194112 | bytes 5636096 | tf_op jit(solution)/shard_map/dot_general | solution.py:29
  150.8 3.8 %all-to-all-done.3.sums_ref = f32[32,1,512]{2,1,0:T(1,128)S(1)} async-done(((f32[32,1,512]{2,1,0:T(1,128)}), f32[32,1,512]{2,1,0:T(1,128)S(1)}, u32[]{:S(2)}, u32[]{:S(2)}) %all-to-all-start.3) | async-done | bytes 65568 | tf_op jit(solution)/shard_map/all_to_all | solution.py:355
  154.6 3.1 %shard_map.62 = (bf16[1024,896]{1,0:T(8,128)(2,1)}, f32[64,896]{1,0:T(8,128)}) custom-call(s32[5]{0:T(128)S(1)} %stack.227.place_ref, bf16[1024,512]{1,0:T(8,128)(2,1)S(1)} %add_convert_fusion.1.left_ref, bf16[512,896]{1,0:T(8,128)(2,1)S(1)} %get-tuple-element.40.right_ref, f32[64,896]{1,0:T(8,128)S(1)} %get-tuple-element.41.own_ref, ...), custom_call_target="tpu_custom_call" | custom-call | flops 939524096 | bytes 4194304 | tf_op jit(solution)/shard_map/pallas_call | solution.py:259
  (65 shorter events, 9.9 us)
Async XLA Ops:
  1.6 11.6 %collective-permute-start.3 = (bf16[64,896]{1,0:T(8,128)(2,1)S(1)}, bf16[64,896]{1,0:T(8,128)(2,1)S(1)}, u32[]{:S(2)}, u32[]{:S(2)}) collective-permute-start(bf16[64,896]{1,0:T(8,128)(2,1)S(1)} %convert_bitcast_fusion.refs_0_), channel_id=1, source_target_pairs={{0,128},{128,0},{1,129},{129,1},{2,130},{130,2},{3,131},{131,3},{4... | collective-permute-start | bytes 344072 | tf_op jit(solution)/shard_map/ppermute | solution.py:281
  9.4 7.2 %collective-permute-start = (bf16[64,896]{1,0:T(8,128)(2,1)S(1)}, bf16[64,896]{1,0:T(8,128)(2,1)S(1)}, u32[]{:S(2)}, u32[]{:S(2)}) collective-permute-start(bf16[64,896]{1,0:T(8,128)(2,1)S(1)} %convert_bitcast_fusion.refs_0_), channel_id=1, source_target_pairs={{0,96},{32,0},{64,32},{96,64},{1,97},{33,1},{65,33},{97,65},{2,98}... | collective-permute-start | bytes 344072 | tf_op jit(solution)/shard_map/ppermute | solution.py:281
  12.1 8.3 %collective-permute-start.1 = (bf16[64,896]{1,0:T(8,128)(2,1)S(1)}, bf16[64,896]{1,0:T(8,128)(2,1)S(1)}, u32[]{:S(2)}, u32[]{:S(2)}) collective-permute-start(bf16[64,896]{1,0:T(8,128)(2,1)S(1)} %convert_bitcast_fusion.refs_0_), channel_id=1, source_target_pairs={{0,64},{32,96},{64,0},{96,32},{1,65},{33,97},{65,1},{97,33},{2,66}... | collective-permute-start | bytes 344072 | tf_op jit(solution)/shard_map/ppermute | solution.py:281
  12.5 9.1 %collective-permute-start.2 = (bf16[64,896]{1,0:T(8,128)(2,1)S(1)}, bf16[64,896]{1,0:T(8,128)(2,1)S(1)}, u32[]{:S(2)}, u32[]{:S(2)}) collective-permute-start(bf16[64,896]{1,0:T(8,128)(2,1)S(1)} %convert_bitcast_fusion.refs_0_), channel_id=1, source_target_pairs={{0,32},{32,64},{64,96},{96,0},{1,33},{33,65},{65,97},{97,1},{2,34}... | collective-permute-start | bytes 344072 | tf_op jit(solution)/shard_map/ppermute | solution.py:281
  13.2 8.4 %collective-permute-start.4 = (bf16[64,896]{1,0:T(8,128)(2,1)S(1)}, bf16[64,896]{1,0:T(8,128)(2,1)S(1)}, u32[]{:S(2)}, u32[]{:S(2)}) collective-permute-start(bf16[64,896]{1,0:T(8,128)(2,1)S(1)} %collective-permute-done.3.refs_4_), channel_id=1, source_target_pairs={{0,96},{32,0},{64,32},{96,64},{1,97},{33,1},{65,33},{97,65},{2,98}... | collective-permute-start | bytes 344072 | tf_op jit(solution)/shard_map/ppermute | solution.py:281
  15.2 6.5 %collective-permute-start.5 = (bf16[64,896]{1,0:T(8,128)(2,1)S(1)}, bf16[64,896]{1,0:T(8,128)(2,1)S(1)}, u32[]{:S(2)}, u32[]{:S(2)}) collective-permute-start(bf16[64,896]{1,0:T(8,128)(2,1)S(1)} %collective-permute-done.3.refs_4_), channel_id=1, source_target_pairs={{0,64},{32,96},{64,0},{96,32},{1,65},{33,97},{65,1},{97,33},{2,66}... | collective-permute-start | bytes 344072 | tf_op jit(solution)/shard_map/ppermute | solution.py:281
  16.6 7.8 %collective-permute-start.6 = (bf16[64,896]{1,0:T(8,128)(2,1)S(1)}, bf16[64,896]{1,0:T(8,128)(2,1)S(1)}, u32[]{:S(2)}, u32[]{:S(2)}) collective-permute-start(bf16[64,896]{1,0:T(8,128)(2,1)S(1)} %collective-permute-done.3.refs_4_), channel_id=1, source_target_pairs={{0,32},{32,64},{64,96},{96,0},{1,33},{33,65},{65,97},{97,1},{2,34}... | collective-permute-start | bytes 344072 | tf_op jit(solution)/shard_map/ppermute | solution.py:281
  20.4 4.6 %copy-start = (bf16[1024,896]{1,0:T(8,128)(2,1)S(1)}, bf16[1024,896]{1,0:T(8,128)(2,1)}, u32[]{:S(2)}) copy-start(bf16[1024,896]{1,0:T(8,128)(2,1)} %add_convert_fusion) | copy-start | bytes 5505028
  25.8 4.2 %collective-permute-start.7 = (bf16[512,512]{1,0:T(8,128)(2,1)S(1)}, bf16[512,512]{1,0:T(8,128)(2,1)S(1)}, u32[]{:S(2)}, u32[]{:S(2)}) collective-permute-start(bf16[512,512]{1,0:T(8,128)(2,1)S(1)} %convolution_convert_fusion.1), channel_id=1, source_target_pairs={{0,1},{1,0},{2,3},{3,2},{4,5},{5,4},{6,7},{7,6},{8,9},{9,8},{10,11... | collective-permute-start | bytes 1572872 | tf_op jit(solution)/shard_map/ppermute | solution.py:281
  30.2 6.3 %collective-permute-start.10 = (bf16[128,512]{1,0:T(8,128)(2,1)S(1)}, bf16[128,512]{1,0:T(8,128)(2,1)S(1)}, u32[]{:S(2)}, u32[]{:S(2)}) collective-permute-start(bf16[128,512]{1,0:T(8,128)(2,1)S(1)} %get-tuple-element.50), channel_id=1, source_target_pairs={{0,8},{8,16},{16,24},{24,0},{1,9},{9,17},{17,25},{25,1},{2,10},{10... | collective-permute-start | bytes 393224 | tf_op jit(solution)/shard_map/ppermute | solution.py:281
  31.5 8.8 %collective-permute-start.9 = (bf16[128,512]{1,0:T(8,128)(2,1)S(1)}, bf16[128,512]{1,0:T(8,128)(2,1)S(1)}, u32[]{:S(2)}, u32[]{:S(2)}) collective-permute-start(bf16[128,512]{1,0:T(8,128)(2,1)S(1)} %get-tuple-element.51), channel_id=1, source_target_pairs={{0,16},{8,24},{16,0},{24,8},{1,17},{9,25},{17,1},{25,9},{2,18},{10... | collective-permute-start | bytes 393224 | tf_op jit(solution)/shard_map/ppermute | solution.py:281
  33.9 6.4 %collective-permute-start.8 = (bf16[128,512]{1,0:T(8,128)(2,1)S(1)}, bf16[128,512]{1,0:T(8,128)(2,1)S(1)}, u32[]{:S(2)}, u32[]{:S(2)}) collective-permute-start(bf16[128,512]{1,0:T(8,128)(2,1)S(1)} %get-tuple-element.49), channel_id=1, source_target_pairs={{0,24},{8,0},{16,8},{24,16},{1,25},{9,1},{17,9},{25,17},{2,26},{10... | collective-permute-start | bytes 393224 | tf_op jit(solution)/shard_map/ppermute | solution.py:281
  40.4 4.8 %collective-permute-start.13 = (bf16[32,512]{1,0:T(8,128)(2,1)S(1)}, bf16[32,512]{1,0:T(8,128)(2,1)S(1)}, u32[]{:S(2)}, u32[]{:S(2)}) collective-permute-start(bf16[32,512]{1,0:T(8,128)(2,1)S(1)} %get-tuple-element.53), channel_id=1, source_target_pairs={{0,2},{2,4},{4,6},{6,0},{1,3},{3,5},{5,7},{7,1},{8,10},{10,12},{12... | collective-permute-start | bytes 98312 | tf_op jit(solution)/shard_map/ppermute | solution.py:281
  41.3 4.0 %collective-permute-start.12 = (bf16[32,512]{1,0:T(8,128)(2,1)S(1)}, bf16[32,512]{1,0:T(8,128)(2,1)S(1)}, u32[]{:S(2)}, u32[]{:S(2)}) collective-permute-start(bf16[32,512]{1,0:T(8,128)(2,1)S(1)} %get-tuple-element.54), channel_id=1, source_target_pairs={{0,4},{2,6},{4,0},{6,2},{1,5},{3,7},{5,1},{7,3},{8,12},{10,14},{12... | collective-permute-start | bytes 98312 | tf_op jit(solution)/shard_map/ppermute | solution.py:281
  42.6 3.3 %collective-permute-start.11 = (bf16[32,512]{1,0:T(8,128)(2,1)S(1)}, bf16[32,512]{1,0:T(8,128)(2,1)S(1)}, u32[]{:S(2)}, u32[]{:S(2)}) collective-permute-start(bf16[32,512]{1,0:T(8,128)(2,1)S(1)} %get-tuple-element.52), channel_id=1, source_target_pairs={{0,6},{2,0},{4,2},{6,4},{1,7},{3,1},{5,3},{7,5},{8,14},{10,8},{12,... | collective-permute-start | bytes 98312 | tf_op jit(solution)/shard_map/ppermute | solution.py:281
  55.3 5.0 %collective-permute-start.16 = (bf16[128,512]{1,0:T(8,128)(2,1)S(1)}, bf16[128,512]{1,0:T(8,128)(2,1)S(1)}, u32[]{:S(2)}, u32[]{:S(2)}) collective-permute-start(bf16[128,512]{1,0:T(8,128)(2,1)S(1)} %bitcast.70), channel_id=1, source_target_pairs={{0,8},{8,16},{16,24},{24,0},{1,9},{9,17},{17,25},{25,1},{2,10},{10... | collective-permute-start | bytes 393224 | tf_op jit(solution)/shard_map/ppermute | solution.py:281
  56.1 6.1 %collective-permute-start.15 = (bf16[128,512]{1,0:T(8,128)(2,1)S(1)}, bf16[128,512]{1,0:T(8,128)(2,1)S(1)}, u32[]{:S(2)}, u32[]{:S(2)}) collective-permute-start(bf16[128,512]{1,0:T(8,128)(2,1)S(1)} %bitcast.71), channel_id=1, source_target_pairs={{0,16},{8,24},{16,0},{24,8},{1,17},{9,25},{17,1},{25,9},{2,18},{10... | collective-permute-start | bytes 393224 | tf_op jit(solution)/shard_map/ppermute | solution.py:281
  58.5 3.8 %collective-permute-start.14 = (bf16[128,512]{1,0:T(8,128)(2,1)S(1)}, bf16[128,512]{1,0:T(8,128)(2,1)S(1)}, u32[]{:S(2)}, u32[]{:S(2)}) collective-permute-start(bf16[128,512]{1,0:T(8,128)(2,1)S(1)} %bitcast.72), channel_id=1, source_target_pairs={{0,24},{8,0},{16,8},{24,16},{1,25},{9,1},{17,9},{25,17},{2,26},{10... | collective-permute-start | bytes 393224 | tf_op jit(solution)/shard_map/ppermute | solution.py:281
  62.3 7.3 %collective-permute-start.17 = (bf16[512,512]{1,0:T(8,128)(2,1)S(1)}, bf16[512,512]{1,0:T(8,128)(2,1)S(1)}, u32[]{:S(2)}, u32[]{:S(2)}) collective-permute-start(bf16[512,512]{1,0:T(8,128)(2,1)S(1)} %pad_maximum_fusion.refs_0_), channel_id=1, source_target_pairs={{0,1},{1,0},{2,3},{3,2},{4,5},{5,4},{6,7},{7,6},{8,9},{9,8},{10,11... | collective-permute-start | bytes 1572872 | tf_op jit(solution)/shard_map/ppermute | solution.py:281
  71.5 15.8 %all-to-all-start.1 = ((f32[8,40,128]{2,1,0:T(8,128)}), f32[8,40,128]{2,1,0:T(8,128)S(1)}, u32[]{:S(2)}, u32[]{:S(2)}) async-start(f32[8,40,128]{2,1,0:T(8,128)} %broadcast_in_dim.7), calls=%async_computation.1 | async-start | bytes 327680 | tf_op jit(solution)/shard_map/all_to_all | solution.py:276
  81.2 11.2 %collective-permute-start.18 = (bf16[128,896]{1,0:T(8,128)(2,1)S(1)}, bf16[128,896]{1,0:T(8,128)(2,1)S(1)}, u32[]{:S(2)}, u32[]{:S(2)}) collective-permute-start(bf16[128,896]{1,0:T(8,128)(2,1)S(1)} %get-tuple-element.47), channel_id=1, source_target_pairs={{0,96},{32,0},{64,32},{96,64},{1,97},{33,1},{65,33},{97,65},{2,98}... | collective-permute-start | bytes 688136 | tf_op jit(solution)/shard_map/ppermute | solution.py:281
  83.9 8.4 %collective-permute-start.19 = (bf16[128,896]{1,0:T(8,128)(2,1)S(1)}, bf16[128,896]{1,0:T(8,128)(2,1)S(1)}, u32[]{:S(2)}, u32[]{:S(2)}) collective-permute-start(bf16[128,896]{1,0:T(8,128)(2,1)S(1)} %get-tuple-element.46), channel_id=1, source_target_pairs={{0,64},{32,96},{64,0},{96,32},{1,65},{33,97},{65,1},{97,33},{2,66}... | collective-permute-start | bytes 688136 | tf_op jit(solution)/shard_map/ppermute | solution.py:281
  84.5 13.8 %collective-permute-start.20 = (bf16[128,896]{1,0:T(8,128)(2,1)S(1)}, bf16[128,896]{1,0:T(8,128)(2,1)S(1)}, u32[]{:S(2)}, u32[]{:S(2)}) collective-permute-start(bf16[128,896]{1,0:T(8,128)(2,1)S(1)} %get-tuple-element.45), channel_id=1, source_target_pairs={{0,32},{32,64},{64,96},{96,0},{1,33},{33,65},{65,97},{97,1},{2,34}... | collective-permute-start | bytes 688136 | tf_op jit(solution)/shard_map/ppermute | solution.py:281
  87.9 10.4 %all-to-all-start.2 = ((f32[4,40,128]{2,1,0:T(8,128)}), f32[4,40,128]{2,1,0:T(8,128)S(1)}, u32[]{:S(2)}, u32[]{:S(2)}) async-start(f32[4,40,128]{2,1,0:T(8,128)} %broadcast_in_dim.8), calls=%async_computation.2 | async-start | bytes 163840 | tf_op jit(solution)/shard_map/all_to_all | solution.py:276
  98.4 13.4 %collective-permute-start.21 = (bf16[128,896]{1,0:T(8,128)(2,1)S(1)}, bf16[128,896]{1,0:T(8,128)(2,1)S(1)}, u32[]{:S(2)}, u32[]{:S(2)}) collective-permute-start(bf16[128,896]{1,0:T(8,128)(2,1)S(1)} %add_convert_fusion.4), channel_id=1, source_target_pairs={{0,128},{128,0},{1,129},{129,1},{2,130},{130,2},{3,131},{131,3},{4... | collective-permute-start | bytes 688136 | tf_op jit(solution)/shard_map/ppermute | solution.py:281
  103.2 4.4 %collective-permute-start.22 = (f32[160,128]{1,0:T(8,128)S(1)}, f32[160,128]{1,0:T(8,128)S(1)}, u32[]{:S(2)}, u32[]{:S(2)}) collective-permute-start(f32[160,128]{1,0:T(8,128)S(1)} %bitcast.75), channel_id=1, source_target_pairs={{0,24},{8,0},{16,8},{24,16},{1,25},{9,1},{17,9},{25,17},{2,26},{10... | collective-permute-start | bytes 245768 | tf_op jit(solution)/shard_map/ppermute | solution.py:281
  105.7 5.1 %collective-permute-start.23 = (f32[160,128]{1,0:T(8,128)S(1)}, f32[160,128]{1,0:T(8,128)S(1)}, u32[]{:S(2)}, u32[]{:S(2)}) collective-permute-start(f32[160,128]{1,0:T(8,128)S(1)} %bitcast.76), channel_id=1, source_target_pairs={{0,16},{8,24},{16,0},{24,8},{1,17},{9,25},{17,1},{25,9},{2,18},{10... | collective-permute-start | bytes 245768 | tf_op jit(solution)/shard_map/ppermute | solution.py:281
  106.4 5.4 %collective-permute-start.24 = (f32[160,128]{1,0:T(8,128)S(1)}, f32[160,128]{1,0:T(8,128)S(1)}, u32[]{:S(2)}, u32[]{:S(2)}) collective-permute-start(f32[160,128]{1,0:T(8,128)S(1)} %bitcast.77), channel_id=1, source_target_pairs={{0,8},{8,16},{16,24},{24,0},{1,9},{9,17},{17,25},{25,1},{2,10},{10... | collective-permute-start | bytes 245768 | tf_op jit(solution)/shard_map/ppermute | solution.py:281
  111.9 3.3 %collective-permute-start.25 = (f32[640,128]{1,0:T(8,128)S(1)}, f32[640,128]{1,0:T(8,128)S(1)}, u32[]{:S(2)}, u32[]{:S(2)}) collective-permute-start(f32[640,128]{1,0:T(8,128)S(1)} %constant_dynamic-update-slice_fusion.own_ref), channel_id=1, source_target_pairs={{0,1},{1,0},{2,3},{3,2},{4,5},{5,4},{6,7},{7,6},{8,9},{9,8},{10,11... | collective-permute-start | bytes 983048 | tf_op jit(solution)/shard_map/ppermute | solution.py:281
  115.2 21.3 %collective-permute-start.26 = (bf16[128,896]{1,0:T(8,128)(2,1)S(1)}, bf16[128,896]{1,0:T(8,128)(2,1)S(1)}, u32[]{:S(2)}, u32[]{:S(2)}) collective-permute-start(bf16[128,896]{1,0:T(8,128)(2,1)S(1)} %add_convert_fusion.3.refs_0_), channel_id=1, source_target_pairs={{0,96},{32,0},{64,32},{96,64},{1,97},{33,1},{65,33},{97,65},{2,98}... | collective-permute-start | bytes 688136 | tf_op jit(solution)/shard_map/ppermute | solution.py:281
  115.3 21.2 %collective-permute-start.27 = (bf16[128,896]{1,0:T(8,128)(2,1)S(1)}, bf16[128,896]{1,0:T(8,128)(2,1)S(1)}, u32[]{:S(2)}, u32[]{:S(2)}) collective-permute-start(bf16[128,896]{1,0:T(8,128)(2,1)S(1)} %add_convert_fusion.3.refs_0_), channel_id=1, source_target_pairs={{0,64},{32,96},{64,0},{96,32},{1,65},{33,97},{65,1},{97,33},{2,66}... | collective-permute-start | bytes 688136 | tf_op jit(solution)/shard_map/ppermute | solution.py:281
  116.4 20.1 %collective-permute-start.28 = (bf16[128,896]{1,0:T(8,128)(2,1)S(1)}, bf16[128,896]{1,0:T(8,128)(2,1)S(1)}, u32[]{:S(2)}, u32[]{:S(2)}) collective-permute-start(bf16[128,896]{1,0:T(8,128)(2,1)S(1)} %add_convert_fusion.3.refs_0_), channel_id=1, source_target_pairs={{0,32},{32,64},{64,96},{96,0},{1,33},{33,65},{65,97},{97,1},{2,34}... | collective-permute-start | bytes 688136 | tf_op jit(solution)/shard_map/ppermute | solution.py:281
  139.2 15.4 %all-to-all-start.3 = ((f32[32,1,512]{2,1,0:T(1,128)}), f32[32,1,512]{2,1,0:T(1,128)S(1)}, u32[]{:S(2)}, u32[]{:S(2)}) async-start(f32[32,1,512]{2,1,0:T(1,128)} %get-tuple-element.42), calls=%async_computation.3 | async-start | bytes 131072 | tf_op jit(solution)/shard_map/all_to_all | solution.py:355

commit v3 on v2

--- a/solution.py
+++ b/solution.py
@@ -300,9 +300,9 @@
     z_hi, y, x, z_lo, core = (lax.axis_index(name) for name in ("z_hi", "y", "x", "z_lo", "core"))
     columns = factor.shape[1]
     gram_place = jnp.stack(
-        [(core + c) % 2 * FAR + (x + j) % 4 * 4 + i for c in range(2) for j in range(4) for i in range(4)]
+        [(core + c) % 2 * FAR + (x + j) % 4 * 4 + (z_lo + i) % 4 for c in range(2) for j in range(4) for i in range(4)]
     ).astype(jnp.int32)
-    left_place = jnp.stack([(core + c) % 2 * 4 + (x + j) % 4 for c in range(2) for j in range(4)]).astype(jnp.int32)
+    core_place = jnp.stack([core, 1 - core]).astype(jnp.int32)
     fsdp_place = jnp.stack([(z_hi + h) % 2 * 4 + (y + k) % 4 for h in range(2) for k in range(4)]).astype(jnp.int32)
     row_group = z_hi * 4 + y
     right_place = jnp.stack([(y + k) % 4 for k in range(4)] + [row_group]).astype(jnp.int32)
@@ -322,8 +322,7 @@
     partial_left = (kept + arrived.astype(f32)).astype(bf16)
     left_line = total(exchanged(partial_left, "x", x)).astype(bf16)
     left_rows = total(exchanged(left_line, "z_lo", z_lo)).astype(bf16)
-    left_line = from_everyone(left_rows, "z_lo").reshape(half // 4, R)
-    own_left = jnp.concatenate(ahead(left_line, "x"))
+    own_left = from_everyone(left_rows, ("x", "z_lo")).reshape(half, R)
     other_left = from_ahead(own_left, "core", 1)
 
     local_gram = product(own_left, own_left, 0, 0) + product(other_left, other_left, 0, 0)
@@ -333,11 +332,11 @@
     piece = lax.dynamic_slice_in_dim(packed, (core * FAR + x * 4 + z_lo) * SHARE, SHARE, 0)
     summed = jnp.sum(from_everyone(piece, ("z_hi", "y")), axis=0)
 
-    left_factor = arrange(left_place, (own_left, other_left), half // 4)
+    left_factor = arrange(core_place, (own_left, other_left), half)
     partial_right = product(left_factor, blended, 0, 0).astype(bf16)
     received = exchanged(partial_right, "y", y)
 
-    gram_line = from_everyone(summed, "z_lo").reshape(4 * SHARE, BLOCK)
+    gram_line = jnp.concatenate(ahead(summed, "z_lo"))
     gram_line, *received = lax.optimization_barrier((gram_line, *received))
     right_rows = total(received).astype(bf16)
     gram_line, right_rows = lax.optimization_barrier((gram_line, right_rows))

time: 158 us -> 158 us (level)
  starting transfers between devices: 70.2 us -> 55.9 us
  blocking collectives: 9.39 us -> 21.7 us
  waiting for transfers between devices: 32.8 us -> 35.4 us
    all_to_all x1, blocking collectives: 9.39 us -> 21.7 us  [from_everyone(): lax.all_to_all(jnp.broadcast_to(value[None], (length, *value.shape)), axi...]
    ppermute x29, starting transfers between devices: 52 us -> 45.3 us  [from_ahead(): lax.ppermute(value, axis, [(i, (i - steps) % length) for i in range(lengt...]
    all_to_all x2 -> x1, starting transfers between devices: 10.6 us -> 6.16 us  [from_everyone(): lax.all_to_all(jnp.broadcast_to(value[None], (length, *value.shape)), axi...]
    all_to_all x1, starting transfers between devices: 7.6 us -> 4.43 us  [on_device(): sums = lax.all_to_all(own_sums, TENSOR, 0, 0, tiled=True)]
    ppermute x29, waiting for transfers between devices: 26.8 us -> 29.4 us  [from_ahead(): lax.ppermute(value, axis, [(i, (i - steps) % length) for i in range(lengt...]
  transfers between devices with their start and end apart: 32 -> 31, of which waited for: 19 -> 20; matrix products, arithmetic and copies ran while one was open for 10% -> 9% of each run, Pallas kernels for 12% -> 12%
where the time goes in v3:
time: 158 us
  starting transfers between devices  55.9 us (35%)
  waiting for transfers between devices  35.4 us (22%)
  Pallas kernels  25.3 us (16%)
  blocking collectives  21.7 us (14%)
  matrix products  11.8 us (7%)
  other arithmetic  5.22 us (3%)
    ppermute x29, starting transfers between devices, from_ahead(): lax.ppermute(value, axis, [(i, (i - steps) % length) for i in range(lengt...  45.3 us
    ppermute x29, waiting for transfers between devices, from_ahead(): lax.ppermute(value, axis, [(i, (i - steps) % length) for i in range(lengt...  29.4 us
    pallas_call x4, Pallas kernels, kernel_call(): pl.pallas_call(kernel, out_shape=outputs, in_specs=[pl.BlockSpec(memory_s...  22.2 us
    all_to_all x1, blocking collectives, from_everyone(): lax.all_to_all(jnp.broadcast_to(value[None], (length, *value.shape)), axi...  21.7 us
    dot_general x8, matrix products, product(): lax.dot_general(left, right, (((left_dim,), (right_dim,)), ((), ())), pre...  11.8 us
    all_to_all x1, starting transfers between devices, from_everyone(): lax.all_to_all(jnp.broadcast_to(value[None], (length, *value.shape)), axi...  6.16 us
    all_to_all x1, starting transfers between devices, on_device(): sums = lax.all_to_all(own_sums, TENSOR, 0, 0, tiled=True)  4.43 us
    all_to_all x1, waiting for transfers between devices, on_device(): sums = lax.all_to_all(own_sums, TENSOR, 0, 0, tiled=True)  3.88 us
  transfers between devices with their start and end apart: 31, of which 20 were waited for; matrix products, arithmetic and copies ran while one was open for 9% of the time, Pallas kernels for 12%

profile of v3, /device:TPU:1, one launch (start us, length us, event | category | flops | bytes accessed | tf_op | source)
XLA Modules:
  0.0 157.6 jit_solution(10264305818401980734)
XLA Ops:
  0.6 1.0 convert_bitcast_fusion.refs_0_
  1.6 7.8 %collective-permute-start.3 = (bf16[64,896]{1,0:T(8,128)(2,1)S(1)}, bf16[64,896]{1,0:T(8,128)(2,1)S(1)}, u32[]{:S(2)}, u32[]{:S(2)}) collective-permute-start(bf16[64,896]{1,0:T(8,128)(2,1)S(1)} %convert_bitcast_fusion.refs_0_), channel_id=1, source_target_pairs={{0,128},{128,0},{1,129},{129,1},{2,130},{130,2},{3,131},{131,3},{4... | collective-permute-start | bytes 344072 | tf_op jit(solution)/shard_map/ppermute | solution.py:281
  9.4 2.7 %collective-permute-start = (bf16[64,896]{1,0:T(8,128)(2,1)S(1)}, bf16[64,896]{1,0:T(8,128)(2,1)S(1)}, u32[]{:S(2)}, u32[]{:S(2)}) collective-permute-start(bf16[64,896]{1,0:T(8,128)(2,1)S(1)} %convert_bitcast_fusion.refs_0_), channel_id=1, source_target_pairs={{0,96},{32,0},{64,32},{96,64},{1,97},{33,1},{65,33},{97,65},{2,98}... | collective-permute-start | bytes 344072 | tf_op jit(solution)/shard_map/ppermute | solution.py:281
  12.5 0.7 collective-permute-start.2
  13.2 2.0 %collective-permute-start.4 = (bf16[64,896]{1,0:T(8,128)(2,1)S(1)}, bf16[64,896]{1,0:T(8,128)(2,1)S(1)}, u32[]{:S(2)}, u32[]{:S(2)}) collective-permute-start(bf16[64,896]{1,0:T(8,128)(2,1)S(1)} %collective-permute-done.3.refs_4_), channel_id=1, source_target_pairs={{0,96},{32,0},{64,32},{96,64},{1,97},{33,1},{65,33},{97,65},{2,98}... | collective-permute-start | bytes 344072 | tf_op jit(solution)/shard_map/ppermute | solution.py:281
  15.2 1.4 collective-permute-start.5
  16.6 3.7 %add_convert_fusion = bf16[1024,896]{1,0:T(8,128)(2,1)} fusion(bf16[1024,896]{1,0:T(8,128)(2,1)} %param.4, bf16[1024,896]{1,0:T(8,128)(2,1)} %param.3), kind=kLoop, calls=%fused_computation.1 | loop fusion | flops 3670016 | bytes 5505024 | tf_op jit(solution)/shard_map/convert_element_type | solution.py:314
  20.4 1.1 collective-permute-done.2.refs_3_
  21.7 2.8 %collective-permute-done.6.refs_7_ = bf16[64,896]{1,0:T(8,128)(2,1)S(1)} collective-permute-done((bf16[64,896]{1,0:T(8,128)(2,1)S(1)}, bf16[64,896]{1,0:T(8,128)(2,1)S(1)}, u32[]{:S(2)}, u32[]{:S(2)}) %collective-permute-start.6) | collective-permute-done | bytes 114720 | tf_op jit(solution)/shard_map/ppermute | solution.py:281
  25.1 0.7 convolution_convert_fusion.1
  25.8 2.2 %collective-permute-start.7 = (bf16[512,512]{1,0:T(8,128)(2,1)S(1)}, bf16[512,512]{1,0:T(8,128)(2,1)S(1)}, u32[]{:S(2)}, u32[]{:S(2)}) collective-permute-start(bf16[512,512]{1,0:T(8,128)(2,1)S(1)} %convolution_convert_fusion.1), channel_id=1, source_target_pairs={{0,1},{1,0},{2,3},{3,2},{4,5},{5,4},{6,7},{7,6},{8,9},{9,8},{10,11... | collective-permute-start | bytes 1572872 | tf_op jit(solution)/shard_map/ppermute | solution.py:281
  28.1 1.9 %fusion.1 = f32[512,512]{1,0:T(8,128)S(1)} fusion(bf16[512,896]{1,0:T(8,128)(2,1)S(1)} %shard_map.58, bf16[1024,896]{1,0:T(8,128)(2,1)} %add_convert_fusion, s32[]{:T(128)S(6)} %select_n.336), kind=kOutput, calls=%fused_computation.9 | convolution fusion | flops 469762048 | bytes 2883588 | tf_op jit(solution)/shard_map/dot_general | solution.py:29
  30.2 1.3 collective-permute-start.10
  31.5 2.5 %collective-permute-start.9 = (bf16[128,512]{1,0:T(8,128)(2,1)S(1)}, bf16[128,512]{1,0:T(8,128)(2,1)S(1)}, u32[]{:S(2)}, u32[]{:S(2)}) collective-permute-start(bf16[128,512]{1,0:T(8,128)(2,1)S(1)} %get-tuple-element.51), channel_id=1, source_target_pairs={{0,16},{8,24},{16,0},{24,8},{1,17},{9,25},{17,1},{25,9},{2,18},{10... | collective-permute-start | bytes 393224 | tf_op jit(solution)/shard_map/ppermute | solution.py:281
  33.9 1.2 collective-permute-start.8
  35.1 1.4 collective-permute-done.10
  36.5 3.8 %collective-permute-done.9 = bf16[128,512]{1,0:T(8,128)(2,1)S(1)} collective-permute-done((bf16[128,512]{1,0:T(8,128)(2,1)S(1)}, bf16[128,512]{1,0:T(8,128)(2,1)S(1)}, u32[]{:S(2)}, u32[]{:S(2)}) %collective-permute-start.9) | collective-permute-done | bytes 131104 | tf_op jit(solution)/shard_map/ppermute | solution.py:281
  40.4 0.8 collective-permute-start.13
  41.3 1.3 collective-permute-start.12
  42.6 2.3 %collective-permute-start.11 = (bf16[32,512]{1,0:T(8,128)(2,1)S(1)}, bf16[32,512]{1,0:T(8,128)(2,1)S(1)}, u32[]{:S(2)}, u32[]{:S(2)}) collective-permute-start(bf16[32,512]{1,0:T(8,128)(2,1)S(1)} %get-tuple-element.52), channel_id=1, source_target_pairs={{0,6},{2,0},{4,2},{6,4},{1,7},{3,1},{5,3},{7,5},{8,14},{10,8},{12,... | collective-permute-start | bytes 98312 | tf_op jit(solution)/shard_map/ppermute | solution.py:281
  45.9 21.7 %all_to_all.15 = bf16[16,32,512]{2,1,0:T(8,128)(2,1)S(1)} all-to-all(bf16[16,32,512]{2,1,0:T(8,128)(2,1)S(1)} %broadcast_in_dim.4), channel_id=1, replica_groups=mesh['z_hi'=2,'y'=4,'x'=4,'z_lo'=4,'core'=2] {'x','z_lo'}, dimensions={0} | all-to-all | bytes 1048576 | tf_op jit(solution)/shard_map/all_to_all | solution.py:276
  67.6 2.4 %collective-permute-start.14 = (bf16[512,512]{1,0:T(8,128)(2,1)S(1)}, bf16[512,512]{1,0:T(8,128)(2,1)S(1)}, u32[]{:S(2)}, u32[]{:S(2)}) collective-permute-start(bf16[512,512]{1,0:T(8,128)(2,1)S(1)} %bitcast.67), channel_id=1, source_target_pairs={{0,1},{1,0},{2,3},{3,2},{4,5},{5,4},{6,7},{7,6},{8,9},{9,8},{10,11... | collective-permute-start | bytes 1572872 | tf_op jit(solution)/shard_map/ppermute | solution.py:281
  70.5 1.0 collective-permute-done.14.refs_1_
  72.2 0.7 broadcast_in_dim.5
  72.9 6.2 %all-to-all-start.1 = ((f32[8,40,128]{2,1,0:T(8,128)}), f32[8,40,128]{2,1,0:T(8,128)S(1)}, u32[]{:S(2)}, u32[]{:S(2)}) async-start(f32[8,40,128]{2,1,0:T(8,128)} %broadcast_in_dim.5), calls=%async_computation.1 | async-start | bytes 327680 | tf_op jit(solution)/shard_map/all_to_all | solution.py:276
  79.6 2.8 %convolution_convert_fusion = bf16[512,896]{1,0:T(8,128)(2,1)S(1)} fusion(bf16[1024,512]{1,0:T(8,128)(2,1)S(1)} %shard_map.59, bf16[1024,896]{1,0:T(8,128)(2,1)} %add_convert_fusion), kind=kOutput, calls=%fused_computation.3 | convolution fusion | flops 939982848 | bytes 3801088 | tf_op jit(solution)/shard_map/dot_general | solution.py:29
  82.5 2.8 %collective-permute-start.18 = (bf16[128,896]{1,0:T(8,128)(2,1)S(1)}, bf16[128,896]{1,0:T(8,128)(2,1)S(1)}, u32[]{:S(2)}, u32[]{:S(2)}) collective-permute-start(bf16[128,896]{1,0:T(8,128)(2,1)S(1)} %get-tuple-element.47), channel_id=1, source_target_pairs={{0,96},{32,0},{64,32},{96,64},{1,97},{33,1},{65,33},{97,65},{2,98}... | collective-permute-start | bytes 688136 | tf_op jit(solution)/shard_map/ppermute | solution.py:281
  86.4 2.1 %all-to-all-done.1 = f32[8,40,128]{2,1,0:T(8,128)S(1)} async-done(((f32[8,40,128]{2,1,0:T(8,128)}), f32[8,40,128]{2,1,0:T(8,128)S(1)}, u32[]{:S(2)}, u32[]{:S(2)}) %all-to-all-start.1) | async-done | bytes 163872 | tf_op jit(solution)/shard_map/all_to_all | solution.py:276
  88.6 1.2 collective-permute-start.17
  89.7 3.6 %collective-permute-done.17 = f32[40,128]{1,0:T(8,128)S(1)} collective-permute-done((f32[40,128]{1,0:T(8,128)S(1)}, f32[40,128]{1,0:T(8,128)S(1)}, u32[]{:S(2)}, u32[]{:S(2)}) %collective-permute-start.17) | collective-permute-done | bytes 20512 | tf_op jit(solution)/shard_map/ppermute | solution.py:281
  93.8 2.5 %collective-permute-done.15 = f32[40,128]{1,0:T(8,128)S(1)} collective-permute-done((f32[40,128]{1,0:T(8,128)S(1)}, f32[40,128]{1,0:T(8,128)S(1)}, u32[]{:S(2)}, u32[]{:S(2)}) %collective-permute-start.15) | collective-permute-done | bytes 20512 | tf_op jit(solution)/shard_map/ppermute | solution.py:281
  96.3 3.3 %collective-permute-done.20 = bf16[128,896]{1,0:T(8,128)(2,1)S(1)} collective-permute-done((bf16[128,896]{1,0:T(8,128)(2,1)S(1)}, bf16[128,896]{1,0:T(8,128)(2,1)S(1)}, u32[]{:S(2)}, u32[]{:S(2)}) %collective-permute-start.20) | collective-permute-done | bytes 229408 | tf_op jit(solution)/shard_map/ppermute | solution.py:281
  99.8 4.7 %collective-permute-start.21 = (bf16[128,896]{1,0:T(8,128)(2,1)S(1)}, bf16[128,896]{1,0:T(8,128)(2,1)S(1)}, u32[]{:S(2)}, u32[]{:S(2)}) collective-permute-start(bf16[128,896]{1,0:T(8,128)(2,1)S(1)} %add_convert_fusion.4), channel_id=1, source_target_pairs={{0,128},{128,0},{1,129},{129,1},{2,130},{130,2},{3,131},{131,3},{4... | collective-permute-start | bytes 688136 | tf_op jit(solution)/shard_map/ppermute | solution.py:281
  106.0 2.1 %collective-permute-done.22 = f32[160,128]{1,0:T(8,128)S(1)} collective-permute-done((f32[160,128]{1,0:T(8,128)S(1)}, f32[160,128]{1,0:T(8,128)S(1)}, u32[]{:S(2)}, u32[]{:S(2)}) %collective-permute-start.22) | collective-permute-done | bytes 81952 | tf_op jit(solution)/shard_map/ppermute | solution.py:281
  108.1 2.1 %collective-permute-done.23 = f32[160,128]{1,0:T(8,128)S(1)} collective-permute-done((f32[160,128]{1,0:T(8,128)S(1)}, f32[160,128]{1,0:T(8,128)S(1)}, u32[]{:S(2)}, u32[]{:S(2)}) %collective-permute-start.23) | collective-permute-done | bytes 81952 | tf_op jit(solution)/shard_map/ppermute | solution.py:281
  110.2 1.1 collective-permute-done.24
  111.3 1.9 %collective-permute-done.21 = bf16[128,896]{1,0:T(8,128)(2,1)S(1)} collective-permute-done((bf16[128,896]{1,0:T(8,128)(2,1)S(1)}, bf16[128,896]{1,0:T(8,128)(2,1)S(1)}, u32[]{:S(2)}, u32[]{:S(2)}) %collective-permute-start.21) | collective-permute-done | bytes 229408 | tf_op jit(solution)/shard_map/ppermute | solution.py:281
  113.3 3.6 %collective-permute-start.25 = (f32[640,128]{1,0:T(8,128)S(1)}, f32[640,128]{1,0:T(8,128)S(1)}, u32[]{:S(2)}, u32[]{:S(2)}) collective-permute-start(f32[640,128]{1,0:T(8,128)S(1)} %constant_dynamic-update-slice_fusion.own_ref), channel_id=1, source_target_pairs={{0,1},{1,0},{2,3},{3,2},{4,5},{5,4},{6,7},{7,6},{8,9},{9,8},{10,11... | collective-permute-start | bytes 983048 | tf_op jit(solution)/shard_map/ppermute | solution.py:281
  117.2 1.0 collective-permute-done.25.other_ref
  118.2 1.5 collective-permute-start.28
  119.6 18.3 %shard_map.60 = (bf16[512,512]{1,0:T(8,128)(2,1)S(1)}, bf16[512,512]{1,0:T(8,128)(2,1)S(1)}) custom-call(s32[32]{0:T(128)S(1)} %stack.197.place_ref, f32[640,128]{1,0:T(8,128)S(1)} %constant_dynamic-update-slice_fusion.own_ref, f32[640,128]{1,0:T(8,128)S(1)} %collective-permute-done.25.other_ref), custom_call_target="tpu_custom_call" | custom-call | flops 2684354560 | bytes 2097152 | tf_op jit(solution)/shard_map/pallas_call | solution.py:162
  137.9 0.7 fusion.5
  138.7 0.7 add_convert_fusion.1.left_ref
  139.5 2.7 %shard_map.61 = (bf16[512,896]{1,0:T(8,128)(2,1)S(1)}, f32[64,896]{1,0:T(8,128)S(1)}, f32[32,1,512]{2,1,0:T(1,128)}) custom-call(s32[5]{0:T(128)S(1)} %stack.203.place_ref, bf16[512,512]{1,0:T(8,128)(2,1)S(1)} %get-tuple-element.37.high_ref, bf16[512,512]{1,0:T(8,128)(2,1)S(1)} %get-tuple-element.38.low_ref, bf16[128,896]{1,0:T(8,128)(2,1)S(1)} %add_convert_fusion.3.refs_0_, ...), custom_call_target="tpu_custom_call" | custom-call | flops 939524096 | bytes 2097152 | tf_op jit(solution)/shard_map/pallas_call | solution.py:162
  142.1 4.4 %all-to-all-start.2 = ((f32[32,1,512]{2,1,0:T(1,128)}), f32[32,1,512]{2,1,0:T(1,128)S(1)}, u32[]{:S(2)}, u32[]{:S(2)}) async-start(f32[32,1,512]{2,1,0:T(1,128)} %get-tuple-element.42), calls=%async_computation.2 | async-start | bytes 131072 | tf_op jit(solution)/shard_map/all_to_all | solution.py:354
  146.6 4.0 %subtract_convert_fusion = bf16[1024,896]{1,0:T(8,128)(2,1)} fusion(bf16[1024,896]{1,0:T(8,128)(2,1)} %add_convert_fusion, bf16[1024,512]{1,0:T(8,128)(2,1)S(1)} %add_convert_fusion.1.left_ref, bf16[512,896]{1,0:T(8,128)(2,1)S(1)} %get-tuple-element.40.right_ref), kind=kOutput, calls=%fused_computation | convolution fusion | flops 943194112 | bytes 5636096 | tf_op jit(solution)/shard_map/dot_general | solution.py:29
  150.6 3.9 %all-to-all-done.2.sums_ref = f32[32,1,512]{2,1,0:T(1,128)S(1)} async-done(((f32[32,1,512]{2,1,0:T(1,128)}), f32[32,1,512]{2,1,0:T(1,128)S(1)}, u32[]{:S(2)}, u32[]{:S(2)}) %all-to-all-start.2) | async-done | bytes 65568 | tf_op jit(solution)/shard_map/all_to_all | solution.py:354
  154.5 3.1 %shard_map.62 = (bf16[1024,896]{1,0:T(8,128)(2,1)}, f32[64,896]{1,0:T(8,128)}) custom-call(s32[5]{0:T(128)S(1)} %stack.203.place_ref, bf16[1024,512]{1,0:T(8,128)(2,1)S(1)} %add_convert_fusion.1.left_ref, bf16[512,896]{1,0:T(8,128)(2,1)S(1)} %get-tuple-element.40.right_ref, f32[64,896]{1,0:T(8,128)S(1)} %get-tuple-element.41.own_ref, ...), custom_call_target="tpu_custom_call" | custom-call | flops 939524096 | bytes 4194304 | tf_op jit(solution)/shard_map/pallas_call | solution.py:259
  (62 shorter events, 7.9 us)
Async XLA Ops:
  1.6 11.6 %collective-permute-start.3 = (bf16[64,896]{1,0:T(8,128)(2,1)S(1)}, bf16[64,896]{1,0:T(8,128)(2,1)S(1)}, u32[]{:S(2)}, u32[]{:S(2)}) collective-permute-start(bf16[64,896]{1,0:T(8,128)(2,1)S(1)} %convert_bitcast_fusion.refs_0_), channel_id=1, source_target_pairs={{0,128},{128,0},{1,129},{129,1},{2,130},{130,2},{3,131},{131,3},{4... | collective-permute-start | bytes 344072 | tf_op jit(solution)/shard_map/ppermute | solution.py:281
  9.4 7.2 %collective-permute-start = (bf16[64,896]{1,0:T(8,128)(2,1)S(1)}, bf16[64,896]{1,0:T(8,128)(2,1)S(1)}, u32[]{:S(2)}, u32[]{:S(2)}) collective-permute-start(bf16[64,896]{1,0:T(8,128)(2,1)S(1)} %convert_bitcast_fusion.refs_0_), channel_id=1, source_target_pairs={{0,96},{32,0},{64,32},{96,64},{1,97},{33,1},{65,33},{97,65},{2,98}... | collective-permute-start | bytes 344072 | tf_op jit(solution)/shard_map/ppermute | solution.py:281
  12.1 8.3 %collective-permute-start.1 = (bf16[64,896]{1,0:T(8,128)(2,1)S(1)}, bf16[64,896]{1,0:T(8,128)(2,1)S(1)}, u32[]{:S(2)}, u32[]{:S(2)}) collective-permute-start(bf16[64,896]{1,0:T(8,128)(2,1)S(1)} %convert_bitcast_fusion.refs_0_), channel_id=1, source_target_pairs={{0,64},{32,96},{64,0},{96,32},{1,65},{33,97},{65,1},{97,33},{2,66}... | collective-permute-start | bytes 344072 | tf_op jit(solution)/shard_map/ppermute | solution.py:281
  12.5 9.1 %collective-permute-start.2 = (bf16[64,896]{1,0:T(8,128)(2,1)S(1)}, bf16[64,896]{1,0:T(8,128)(2,1)S(1)}, u32[]{:S(2)}, u32[]{:S(2)}) collective-permute-start(bf16[64,896]{1,0:T(8,128)(2,1)S(1)} %convert_bitcast_fusion.refs_0_), channel_id=1, source_target_pairs={{0,32},{32,64},{64,96},{96,0},{1,33},{33,65},{65,97},{97,1},{2,34}... | collective-permute-start | bytes 344072 | tf_op jit(solution)/shard_map/ppermute | solution.py:281
  13.2 8.4 %collective-permute-start.4 = (bf16[64,896]{1,0:T(8,128)(2,1)S(1)}, bf16[64,896]{1,0:T(8,128)(2,1)S(1)}, u32[]{:S(2)}, u32[]{:S(2)}) collective-permute-start(bf16[64,896]{1,0:T(8,128)(2,1)S(1)} %collective-permute-done.3.refs_4_), channel_id=1, source_target_pairs={{0,96},{32,0},{64,32},{96,64},{1,97},{33,1},{65,33},{97,65},{2,98}... | collective-permute-start | bytes 344072 | tf_op jit(solution)/shard_map/ppermute | solution.py:281
  15.2 6.5 %collective-permute-start.5 = (bf16[64,896]{1,0:T(8,128)(2,1)S(1)}, bf16[64,896]{1,0:T(8,128)(2,1)S(1)}, u32[]{:S(2)}, u32[]{:S(2)}) collective-permute-start(bf16[64,896]{1,0:T(8,128)(2,1)S(1)} %collective-permute-done.3.refs_4_), channel_id=1, source_target_pairs={{0,64},{32,96},{64,0},{96,32},{1,65},{33,97},{65,1},{97,33},{2,66}... | collective-permute-start | bytes 344072 | tf_op jit(solution)/shard_map/ppermute | solution.py:281
  16.6 7.8 %collective-permute-start.6 = (bf16[64,896]{1,0:T(8,128)(2,1)S(1)}, bf16[64,896]{1,0:T(8,128)(2,1)S(1)}, u32[]{:S(2)}, u32[]{:S(2)}) collective-permute-start(bf16[64,896]{1,0:T(8,128)(2,1)S(1)} %collective-permute-done.3.refs_4_), channel_id=1, source_target_pairs={{0,32},{32,64},{64,96},{96,0},{1,33},{33,65},{65,97},{97,1},{2,34}... | collective-permute-start | bytes 344072 | tf_op jit(solution)/shard_map/ppermute | solution.py:281
  20.4 4.6 %copy-start = (bf16[1024,896]{1,0:T(8,128)(2,1)S(1)}, bf16[1024,896]{1,0:T(8,128)(2,1)}, u32[]{:S(2)}) copy-start(bf16[1024,896]{1,0:T(8,128)(2,1)} %add_convert_fusion) | copy-start | bytes 5505028
  25.8 4.2 %collective-permute-start.7 = (bf16[512,512]{1,0:T(8,128)(2,1)S(1)}, bf16[512,512]{1,0:T(8,128)(2,1)S(1)}, u32[]{:S(2)}, u32[]{:S(2)}) collective-permute-start(bf16[512,512]{1,0:T(8,128)(2,1)S(1)} %convolution_convert_fusion.1), channel_id=1, source_target_pairs={{0,1},{1,0},{2,3},{3,2},{4,5},{5,4},{6,7},{7,6},{8,9},{9,8},{10,11... | collective-permute-start | bytes 1572872 | tf_op jit(solution)/shard_map/ppermute | solution.py:281
  30.2 6.3 %collective-permute-start.10 = (bf16[128,512]{1,0:T(8,128)(2,1)S(1)}, bf16[128,512]{1,0:T(8,128)(2,1)S(1)}, u32[]{:S(2)}, u32[]{:S(2)}) collective-permute-start(bf16[128,512]{1,0:T(8,128)(2,1)S(1)} %get-tuple-element.50), channel_id=1, source_target_pairs={{0,8},{8,16},{16,24},{24,0},{1,9},{9,17},{17,25},{25,1},{2,10},{10... | collective-permute-start | bytes 393224 | tf_op jit(solution)/shard_map/ppermute | solution.py:281
  31.5 8.8 %collective-permute-start.9 = (bf16[128,512]{1,0:T(8,128)(2,1)S(1)}, bf16[128,512]{1,0:T(8,128)(2,1)S(1)}, u32[]{:S(2)}, u32[]{:S(2)}) collective-permute-start(bf16[128,512]{1,0:T(8,128)(2,1)S(1)} %get-tuple-element.51), channel_id=1, source_target_pairs={{0,16},{8,24},{16,0},{24,8},{1,17},{9,25},{17,1},{25,9},{2,18},{10... | collective-permute-start | bytes 393224 | tf_op jit(solution)/shard_map/ppermute | solution.py:281
  33.9 6.4 %collective-permute-start.8 = (bf16[128,512]{1,0:T(8,128)(2,1)S(1)}, bf16[128,512]{1,0:T(8,128)(2,1)S(1)}, u32[]{:S(2)}, u32[]{:S(2)}) collective-permute-start(bf16[128,512]{1,0:T(8,128)(2,1)S(1)} %get-tuple-element.49), channel_id=1, source_target_pairs={{0,24},{8,0},{16,8},{24,16},{1,25},{9,1},{17,9},{25,17},{2,26},{10... | collective-permute-start | bytes 393224 | tf_op jit(solution)/shard_map/ppermute | solution.py:281
  40.4 4.8 %collective-permute-start.13 = (bf16[32,512]{1,0:T(8,128)(2,1)S(1)}, bf16[32,512]{1,0:T(8,128)(2,1)S(1)}, u32[]{:S(2)}, u32[]{:S(2)}) collective-permute-start(bf16[32,512]{1,0:T(8,128)(2,1)S(1)} %get-tuple-element.53), channel_id=1, source_target_pairs={{0,2},{2,4},{4,6},{6,0},{1,3},{3,5},{5,7},{7,1},{8,10},{10,12},{12... | collective-permute-start | bytes 98312 | tf_op jit(solution)/shard_map/ppermute | solution.py:281
  41.3 4.0 %collective-permute-start.12 = (bf16[32,512]{1,0:T(8,128)(2,1)S(1)}, bf16[32,512]{1,0:T(8,128)(2,1)S(1)}, u32[]{:S(2)}, u32[]{:S(2)}) collective-permute-start(bf16[32,512]{1,0:T(8,128)(2,1)S(1)} %get-tuple-element.54), channel_id=1, source_target_pairs={{0,4},{2,6},{4,0},{6,2},{1,5},{3,7},{5,1},{7,3},{8,12},{10,14},{12... | collective-permute-start | bytes 98312 | tf_op jit(solution)/shard_map/ppermute | solution.py:281
  42.6 3.3 %collective-permute-start.11 = (bf16[32,512]{1,0:T(8,128)(2,1)S(1)}, bf16[32,512]{1,0:T(8,128)(2,1)S(1)}, u32[]{:S(2)}, u32[]{:S(2)}) collective-permute-start(bf16[32,512]{1,0:T(8,128)(2,1)S(1)} %get-tuple-element.52), channel_id=1, source_target_pairs={{0,6},{2,0},{4,2},{6,4},{1,7},{3,1},{5,3},{7,5},{8,14},{10,8},{12,... | collective-permute-start | bytes 98312 | tf_op jit(solution)/shard_map/ppermute | solution.py:281
  67.6 3.9 %collective-permute-start.14 = (bf16[512,512]{1,0:T(8,128)(2,1)S(1)}, bf16[512,512]{1,0:T(8,128)(2,1)S(1)}, u32[]{:S(2)}, u32[]{:S(2)}) collective-permute-start(bf16[512,512]{1,0:T(8,128)(2,1)S(1)} %bitcast.67), channel_id=1, source_target_pairs={{0,1},{1,0},{2,3},{3,2},{4,5},{5,4},{6,7},{7,6},{8,9},{9,8},{10,11... | collective-permute-start | bytes 1572872 | tf_op jit(solution)/shard_map/ppermute | solution.py:281
  72.9 15.7 %all-to-all-start.1 = ((f32[8,40,128]{2,1,0:T(8,128)}), f32[8,40,128]{2,1,0:T(8,128)S(1)}, u32[]{:S(2)}, u32[]{:S(2)}) async-start(f32[8,40,128]{2,1,0:T(8,128)} %broadcast_in_dim.5), calls=%async_computation.1 | async-start | bytes 327680 | tf_op jit(solution)/shard_map/all_to_all | solution.py:276
  82.5 13.8 %collective-permute-start.18 = (bf16[128,896]{1,0:T(8,128)(2,1)S(1)}, bf16[128,896]{1,0:T(8,128)(2,1)S(1)}, u32[]{:S(2)}, u32[]{:S(2)}) collective-permute-start(bf16[128,896]{1,0:T(8,128)(2,1)S(1)} %get-tuple-element.47), channel_id=1, source_target_pairs={{0,96},{32,0},{64,32},{96,64},{1,97},{33,1},{65,33},{97,65},{2,98}... | collective-permute-start | bytes 688136 | tf_op jit(solution)/shard_map/ppermute | solution.py:281
  85.3 11.0 %collective-permute-start.19 = (bf16[128,896]{1,0:T(8,128)(2,1)S(1)}, bf16[128,896]{1,0:T(8,128)(2,1)S(1)}, u32[]{:S(2)}, u32[]{:S(2)}) collective-permute-start(bf16[128,896]{1,0:T(8,128)(2,1)S(1)} %get-tuple-element.46), channel_id=1, source_target_pairs={{0,64},{32,96},{64,0},{96,32},{1,65},{33,97},{65,1},{97,33},{2,66}... | collective-permute-start | bytes 688136 | tf_op jit(solution)/shard_map/ppermute | solution.py:281
  85.8 13.8 %collective-permute-start.20 = (bf16[128,896]{1,0:T(8,128)(2,1)S(1)}, bf16[128,896]{1,0:T(8,128)(2,1)S(1)}, u32[]{:S(2)}, u32[]{:S(2)}) collective-permute-start(bf16[128,896]{1,0:T(8,128)(2,1)S(1)} %get-tuple-element.45), channel_id=1, source_target_pairs={{0,32},{32,64},{64,96},{96,0},{1,33},{33,65},{65,97},{97,1},{2,34}... | collective-permute-start | bytes 688136 | tf_op jit(solution)/shard_map/ppermute | solution.py:281
  88.6 4.8 %collective-permute-start.17 = (f32[40,128]{1,0:T(8,128)S(1)}, f32[40,128]{1,0:T(8,128)S(1)}, u32[]{:S(2)}, u32[]{:S(2)}) collective-permute-start(f32[40,128]{1,0:T(8,128)S(1)} %reduce_sum.9), channel_id=1, source_target_pairs={{0,2},{2,4},{4,6},{6,0},{1,3},{3,5},{5,7},{7,1},{8,10},{10,12},{12... | collective-permute-start | bytes 61448 | tf_op jit(solution)/shard_map/ppermute | solution.py:281
  89.7 4.1 %collective-permute-start.16 = (f32[40,128]{1,0:T(8,128)S(1)}, f32[40,128]{1,0:T(8,128)S(1)}, u32[]{:S(2)}, u32[]{:S(2)}) collective-permute-start(f32[40,128]{1,0:T(8,128)S(1)} %reduce_sum.9), channel_id=1, source_target_pairs={{0,4},{2,6},{4,0},{6,2},{1,5},{3,7},{5,1},{7,3},{8,12},{10,14},{12... | collective-permute-start | bytes 61448 | tf_op jit(solution)/shard_map/ppermute | solution.py:281
  93.4 2.9 %collective-permute-start.15 = (f32[40,128]{1,0:T(8,128)S(1)}, f32[40,128]{1,0:T(8,128)S(1)}, u32[]{:S(2)}, u32[]{:S(2)}) collective-permute-start(f32[40,128]{1,0:T(8,128)S(1)} %reduce_sum.9), channel_id=1, source_target_pairs={{0,6},{2,0},{4,2},{6,4},{1,7},{3,1},{5,3},{7,5},{8,14},{10,8},{12,... | collective-permute-start | bytes 61448 | tf_op jit(solution)/shard_map/ppermute | solution.py:281
  99.8 13.5 %collective-permute-start.21 = (bf16[128,896]{1,0:T(8,128)(2,1)S(1)}, bf16[128,896]{1,0:T(8,128)(2,1)S(1)}, u32[]{:S(2)}, u32[]{:S(2)}) collective-permute-start(bf16[128,896]{1,0:T(8,128)(2,1)S(1)} %add_convert_fusion.4), channel_id=1, source_target_pairs={{0,128},{128,0},{1,129},{129,1},{2,130},{130,2},{3,131},{131,3},{4... | collective-permute-start | bytes 688136 | tf_op jit(solution)/shard_map/ppermute | solution.py:281
  104.5 3.6 %collective-permute-start.22 = (f32[160,128]{1,0:T(8,128)S(1)}, f32[160,128]{1,0:T(8,128)S(1)}, u32[]{:S(2)}, u32[]{:S(2)}) collective-permute-start(f32[160,128]{1,0:T(8,128)S(1)} %pad_maximum_fusion), channel_id=1, source_target_pairs={{0,24},{8,0},{16,8},{24,16},{1,25},{9,1},{17,9},{25,17},{2,26},{10... | collective-permute-start | bytes 245768 | tf_op jit(solution)/shard_map/ppermute | solution.py:281
  105.1 5.1 %collective-permute-start.23 = (f32[160,128]{1,0:T(8,128)S(1)}, f32[160,128]{1,0:T(8,128)S(1)}, u32[]{:S(2)}, u32[]{:S(2)}) collective-permute-start(f32[160,128]{1,0:T(8,128)S(1)} %pad_maximum_fusion), channel_id=1, source_target_pairs={{0,16},{8,24},{16,0},{24,8},{1,17},{9,25},{17,1},{25,9},{2,18},{10... | collective-permute-start | bytes 245768 | tf_op jit(solution)/shard_map/ppermute | solution.py:281
  105.4 6.0 %collective-permute-start.24 = (f32[160,128]{1,0:T(8,128)S(1)}, f32[160,128]{1,0:T(8,128)S(1)}, u32[]{:S(2)}, u32[]{:S(2)}) collective-permute-start(f32[160,128]{1,0:T(8,128)S(1)} %pad_maximum_fusion), channel_id=1, source_target_pairs={{0,8},{8,16},{16,24},{24,0},{1,9},{9,17},{17,25},{25,1},{2,10},{10... | collective-permute-start | bytes 245768 | tf_op jit(solution)/shard_map/ppermute | solution.py:281
  113.3 4.8 %collective-permute-start.25 = (f32[640,128]{1,0:T(8,128)S(1)}, f32[640,128]{1,0:T(8,128)S(1)}, u32[]{:S(2)}, u32[]{:S(2)}) collective-permute-start(f32[640,128]{1,0:T(8,128)S(1)} %constant_dynamic-update-slice_fusion.own_ref), channel_id=1, source_target_pairs={{0,1},{1,0},{2,3},{3,2},{4,5},{5,4},{6,7},{7,6},{8,9},{9,8},{10,11... | collective-permute-start | bytes 983048 | tf_op jit(solution)/shard_map/ppermute | solution.py:281
  118.1 21.3 %collective-permute-start.26 = (bf16[128,896]{1,0:T(8,128)(2,1)S(1)}, bf16[128,896]{1,0:T(8,128)(2,1)S(1)}, u32[]{:S(2)}, u32[]{:S(2)}) collective-permute-start(bf16[128,896]{1,0:T(8,128)(2,1)S(1)} %add_convert_fusion.3.refs_0_), channel_id=1, source_target_pairs={{0,96},{32,0},{64,32},{96,64},{1,97},{33,1},{65,33},{97,65},{2,98}... | collective-permute-start | bytes 688136 | tf_op jit(solution)/shard_map/ppermute | solution.py:281
  118.2 21.3 %collective-permute-start.27 = (bf16[128,896]{1,0:T(8,128)(2,1)S(1)}, bf16[128,896]{1,0:T(8,128)(2,1)S(1)}, u32[]{:S(2)}, u32[]{:S(2)}) collective-permute-start(bf16[128,896]{1,0:T(8,128)(2,1)S(1)} %add_convert_fusion.3.refs_0_), channel_id=1, source_target_pairs={{0,64},{32,96},{64,0},{96,32},{1,65},{33,97},{65,1},{97,33},{2,66}... | collective-permute-start | bytes 688136 | tf_op jit(solution)/shard_map/ppermute | solution.py:281
  118.2 21.3 %collective-permute-start.28 = (bf16[128,896]{1,0:T(8,128)(2,1)S(1)}, bf16[128,896]{1,0:T(8,128)(2,1)S(1)}, u32[]{:S(2)}, u32[]{:S(2)}) collective-permute-start(bf16[128,896]{1,0:T(8,128)(2,1)S(1)} %add_convert_fusion.3.refs_0_), channel_id=1, source_target_pairs={{0,32},{32,64},{64,96},{96,0},{1,33},{33,65},{65,97},{97,1},{2,34}... | collective-permute-start | bytes 688136 | tf_op jit(solution)/shard_map/ppermute | solution.py:281
  142.1 12.3 %all-to-all-start.2 = ((f32[32,1,512]{2,1,0:T(1,128)}), f32[32,1,512]{2,1,0:T(1,128)S(1)}, u32[]{:S(2)}, u32[]{:S(2)}) async-start(f32[32,1,512]{2,1,0:T(1,128)} %get-tuple-element.42), calls=%async_computation.2 | async-start | bytes 131072 | tf_op jit(solution)/shard_map/all_to_all | solution.py:354
